TPU v7x, 1024 devices: a whole 4x4x32 slice. The times are simulated.
1024 devices in a mesh: gx: 4 (over x), gy: 8 (over y, core), gz: 32 (over z).
Axes of the slice: x: 4, y: 4, z: 32, core: 2. Of those that a mesh axis runs over, the one named last changes fastest.
Arguments:
- volume: float32 [1024, 512, 1024], P('gz', 'gx', 'gy'), may hold values from -3.5 to 3.5
Outputs:
- image: float32 [4, 512, 1024], P(None, 'gx', 'gy')
All inputs are finite; a program needn't handle non-finite values.
Results may differ from a plain program's by a relative error of at most 0.0003.
Values sent between devices are 32-bit elements; how exact they have to be, the bound alone decides.
No kernel may reach another device: no remote copies, remote signals or barrier semaphores. Data moves between devices by JAX's collectives and lax.ppermute only.
A program may use at most 64 MiB of HBM per device.

v0:
```python
import jax
import jax.numpy as jnp
from jax import lax
from jax.sharding import PartitionSpec as P


def with_halo(array, sides, width):
    for axis, dim in sides:
        devices, length = (lax.axis_size(axis), array.shape[dim])
        up = [(i, (i + 1) % devices) for i in range(devices - 1)]
        down = [(j, i) for i, j in up]
        last = lax.slice_in_dim(array, length - width, length, axis=dim)
        initial = lax.slice_in_dim(array, 0, width, axis=dim)
        before = lax.ppermute(last, axis, up)
        after = lax.ppermute(initial, axis, down)
        array = jnp.concatenate([before, array, after], axis=dim)
    return array


def carried_in(array, axis, combine, identity):
    devices, index = (lax.axis_size(axis), lax.axis_index(axis))
    everything = lax.all_gather(array, axis)
    start = jnp.broadcast_to(jnp.asarray(identity, array.dtype), array.shape)

    def step(k, before):
        reached = k < index
        new = combine(before, everything[k])
        return jnp.where(reached, new, before)

    return lax.fori_loop(0, devices, step, start)


def shade_block(extended, depth_cells):
    centre = extended[1:-1, 1:-1, 1:-1]
    slope_z = 0.5 * (extended[2:, 1:-1, 1:-1] - extended[:-2, 1:-1, 1:-1])
    slope_x = 0.5 * (extended[1:-1, 2:, 1:-1] - extended[1:-1, :-2, 1:-1])
    slope_y = 0.5 * (extended[1:-1, 1:-1, 2:] - extended[1:-1, 1:-1, :-2])
    facing = (2.0 * slope_z + slope_x + 2.0 * slope_y) / 3.0
    length = jnp.sqrt(slope_z * slope_z + slope_x * slope_x + slope_y * slope_y + 1.0)
    shading = 0.2 + 2.0 * jnp.abs(facing) / length
    thickness = 2.0 * jnp.exp(centre) / depth_cells
    opacity = -jnp.expm1(-thickness)
    weighted = shading * opacity
    colors = (
        jnp.stack(
            [
                jax.nn.sigmoid(2.0 * centre + 1.0),
                jnp.exp(-centre * centre),
                jax.nn.sigmoid(1.0 - 2.0 * centre),
            ]
        )
        * weighted
    )
    return (thickness, colors)


def add_depth(earlier, later):
    return earlier + later


def finish(summed):
    return jnp.concatenate([summed[:3], -jnp.expm1(-summed[3:4])], axis=0)


def per_device(volume):
    depth_cells = volume.shape[0] * lax.axis_size("gz")
    padded = with_halo(volume, (("gz", 0), ("gx", 1), ("gy", 2)), 1)
    thickness, colors = shade_block(padded, depth_cells)
    before = jnp.cumsum(thickness, axis=0) - thickness
    picture = jnp.concatenate(
        [jnp.sum(jnp.exp(-before) * colors, axis=1), jnp.sum(thickness, axis=0)[None]], axis=0
    )
    own_depth = picture[3:4]
    depth_front = carried_in(own_depth, "gz", add_depth, jnp.zeros_like(own_depth))
    contribution = jnp.concatenate([jnp.exp(-depth_front) * picture[:3], own_depth], axis=0)
    summed = lax.psum(contribution, "gz")
    return finish(summed)


def solution(mesh):
    return jax.shard_map(
        per_device,
        mesh=mesh,
        in_specs=(P("gz", "gx", "gy"),),
        out_specs=P(None, "gx", "gy"),
        check_vma=False,
    )
```

profile of v0, /device:TPU:6, one launch (start us, length us, event | category | flops | bytes accessed | tf_op | source)
XLA Modules:
  0.0 492.6 jit_solution(8900577729729273611)
XLA Ops:
  6.5 0.9 fusion.16
  7.4 3.8 collective-permute-start.1
  11.3 1.3 collective-permute-start
  12.6 0.6 collective-permute-done.1
  13.1 1.7 constant_dynamic-update-slice_fusion.1
  14.9 2.5 collective-permute-done
  17.5 2.7 collective-permute-start.2
  20.2 1.3 collective-permute-start.3
  21.5 0.1 collective-permute-done.2
  21.6 4.2 collective-permute-done.3
  25.8 0.2 pad_maximum_fusion
  26.1 2.2 fusion.14
  28.2 2.9 copy.4
  31.2 1.3 collective-permute-start.4
  32.5 1.3 copy.6
  33.8 3.2 collective-permute-start.5
  36.9 2.2 copy.5
  39.1 2.2 copy.7
  41.3 13.9 %negate_multiply_fusion.1 = (f32[32,128,128]{2,1,0:T(8,128)}, f32[1,32,128,128]{3,2,1,0:T(8,128)}, f32[1,32,128,128]{3,2,1,0:T(8,128)}, f32[1,32,128,128]{3,2,1,0:T(8,128)}, f32[128,128]{1,0:T(8,128)}) fusion(f32[34,1,128]{2,1,0:T(1,128)S(1)} %collective-permute-done.2, f32[34,128,128]{2,1,0:T(8,128)} %copy-done.1, ...), kind=kLoop, calls=%fused_computation.22 | loop fusion | flops 23576576 | bytes 12980768 | tf_op jit(solution)/shard_map/mul | solution.py:43
  55.2 0.0 all-reduce.2.cloned.1.call-start
  55.3 0.6 negate_exponential_fusion
  55.9 1.0 copy-done.2
  56.9 0.6 copy-done.3
  57.5 0.6 copy-done.4
  58.2 2.5 fusion.1
  60.7 141.5 %all-gather.3.cloned.1.call-done = f32[4096,128]{1,0:T(8,128)} async-done(((f32[128,128]{1,0:T(8,128)}), f32[4096,128]{1,0:T(8,128)}) %all-gather.3.cloned.1.call-update) | async-done | bytes 2097168 | tf_op jit(solution)/shard_map/all_gather | solution.py:22
  202.1 28.2 %while.14 = (s32[]{:T(128)}, f32[1,128,128]{2,1,0:T(8,128)S(1)}, s32[]{:T(128)}, f32[32,1,128,128]{3,2,1,0:T(8,128)}, s32[]{:T(128)}, /*index=5*/s32[]{:T(128)}) while((s32[]{:T(128)}, f32[1,128,128]{2,1,0:T(8,128)S(1)}, s32[]{:T(128)}, f32[32,1,128,128]{3,2,1,0:T(8,128)}, s32[]{:T(128)}, /*index=5*/s32[]{:T(128)}) %tuple.48), condition=%wide.region_2.3_spmd.clone, body=%wide.region_1.2_spmd.clone.sunk | while | flops 49156 | bytes 196701 | solution.py:30
  202.1 0.9 add_select_fusion.2
  203.0 0.9 add_select_fusion.2
  203.9 0.9 add_select_fusion.2
  204.8 0.9 add_select_fusion.2
  205.7 0.9 add_select_fusion.2
  206.5 0.9 add_select_fusion.2
  207.4 0.9 add_select_fusion.2
  208.3 0.9 add_select_fusion.2
  209.2 0.9 add_select_fusion.2
  210.1 0.9 add_select_fusion.2
  211.0 0.9 add_select_fusion.2
  211.8 0.9 add_select_fusion.2
  212.7 0.9 add_select_fusion.2
  213.6 0.9 add_select_fusion.2
  214.5 0.9 add_select_fusion.2
  215.4 0.9 add_select_fusion.2
  216.3 0.9 add_select_fusion.2
  217.1 0.9 add_select_fusion.2
  218.0 0.9 add_select_fusion.2
  218.9 0.9 add_select_fusion.2
  219.8 0.9 add_select_fusion.2
  220.7 0.9 add_select_fusion.2
  221.6 0.9 add_select_fusion.2
  222.4 0.9 add_select_fusion.2
  223.3 0.9 add_select_fusion.2
  224.2 0.9 add_select_fusion.2
  225.1 0.9 add_select_fusion.2
  226.0 0.9 add_select_fusion.2
  226.9 0.9 add_select_fusion.2
  227.7 0.9 add_select_fusion.2
  228.6 0.9 add_select_fusion.2
  229.5 0.9 add_select_fusion.2
  230.4 0.7 pad_maximum_fusion.11
  231.2 252.0 %all-reduce.2.cloned.1.call-done = f32[4,128,128]{2,1,0:T(8,128)} async-done(((f32[4,128,128]{2,1,0:T(8,128)}), f32[4,128,128]{2,1,0:T(8,128)}) %all-reduce.2.cloned.1.call-update) | async-done | bytes 262160 | tf_op jit(solution)/shard_map/psum | solution.py:76
  483.2 0.9 slice.66
  484.2 0.9 fusion.12
  485.0 0.7 pad_maximum_fusion.12
  (20 shorter events, 0.1 us)
Async XLA Ops:
  6.5 195.6 %all-gather.3.cloned.1.call-start = ((), (), s32[]{:S(2)}) async-start(), calls=%async_computation.1 | async-start | bytes 2162688 | tf_op jit(solution)/shard_map/all_gather | solution.py:22
  7.4 5.7 %collective-permute-start.1 = (f32[1,128,128]{2,1,0:T(8,128)S(1)}, f32[1,128,128]{2,1,0:T(8,128)S(1)}, u32[]{:S(2)}, u32[]{:S(2)}) collective-permute-start(f32[1,128,128]{2,1,0:T(8,128)S(1)} %get-tuple-element.126), channel_id=1, source_target_pairs={{0,1},{1,2},{2,3},{3,4},{4,5},{5,6},{6,7},{7,8},{8,9},{9,10},{10,1... | collective-permute-start | bytes 196616 | tf_op jit(solution)/shard_map/ppermute | solution.py:14
  11.3 6.2 %collective-permute-start = (f32[1,128,128]{2,1,0:T(8,128)S(1)}, f32[1,128,128]{2,1,0:T(8,128)S(1)}, u32[]{:S(2)}, u32[]{:S(2)}) collective-permute-start(f32[1,128,128]{2,1,0:T(8,128)S(1)} %get-tuple-element.125), channel_id=1, source_target_pairs={{1,0},{2,1},{3,2},{4,3},{5,4},{6,5},{7,6},{8,7},{9,8},{10,9},{11,1... | collective-permute-start | bytes 196616 | tf_op jit(solution)/shard_map/ppermute | solution.py:15
  17.4 8.4 %copy-start.1 = (f32[34,128,128]{2,1,0:T(8,128)}, f32[34,128,128]{2,1,0:T(8,128)S(1)}, u32[]{:S(2)}) copy-start(f32[34,128,128]{2,1,0:T(8,128)S(1)} %constant_dynamic-update-slice_fusion) | copy-start | bytes 6684676
  17.5 4.2 collective-permute-start.2
  20.2 5.6 %collective-permute-start.3 = (f32[34,1,128]{2,1,0:T(1,128)S(1)}, f32[34,1,128]{2,1,0:T(1,128)S(1)}, u32[]{:S(2)}, u32[]{:S(2)}) collective-permute-start(f32[34,1,128]{2,1,0:T(1,128)S(1)} %get-tuple-element.118), channel_id=1, source_target_pairs={{0,256},{256,512},{512,768},{1,257},{257,513},{513,769},{2,258},{2... | collective-permute-start | bytes 52232 | tf_op jit(solution)/shard_map/ppermute | solution.py:14
  31.2 5.8 %collective-permute-start.4 = (f32[34,130,1]{1,2,0:T(1,128)S(1)}, f32[34,130,1]{1,2,0:T(1,128)S(1)}, u32[]{:S(2)}, u32[]{:S(2)}) collective-permute-start(f32[34,130,1]{1,2,0:T(1,128)S(1)} %copy.4), channel_id=1, source_target_pairs={{32,0},{64,32},{96,64},{128,96},{160,128},{192,160},{224,192},{33,... | collective-permute-start | bytes 53048 | tf_op jit(solution)/shard_map/ppermute | solution.py:15
  33.8 7.6 %copy-start = (f32[32,128,128]{2,1,0:T(8,128)S(1)}, f32[32,128,128]{2,1,0:T(8,128)}, u32[]{:S(2)}) copy-start(f32[32,128,128]{2,1,0:T(8,128)} %param.3) | copy-start | bytes 6291460
  33.8 5.4 %collective-permute-start.5 = (f32[34,130,1]{1,2,0:T(1,128)S(1)}, f32[34,130,1]{1,2,0:T(1,128)S(1)}, u32[]{:S(2)}, u32[]{:S(2)}) collective-permute-start(f32[34,130,1]{1,2,0:T(1,128)S(1)} %copy.6), channel_id=1, source_target_pairs={{0,32},{32,64},{64,96},{96,128},{128,160},{160,192},{192,224},{1,3... | collective-permute-start | bytes 53048 | tf_op jit(solution)/shard_map/ppermute | solution.py:14
  55.2 428.0 %all-reduce.2.cloned.1.call-start = ((), (), s32[]{:S(2)}) async-start(), calls=%async_computation | async-start | bytes 524288 | tf_op jit(solution)/shard_map/psum | solution.py:76
  55.3 1.6 copy-start.2
  55.3 2.2 copy-start.3
  55.3 2.8 copy-start.4
  58.2 172.3 %copy-start.5 = (f32[128,128]{1,0:T(8,128)S(1)}, f32[128,128]{1,0:T(8,128)}, u32[]{:S(2)}) copy-start(f32[128,128]{1,0:T(8,128)} %get-tuple-element.124) | copy-start | bytes 196612
Sparse Core Ops, SparseCore 0:
  55.4 146.7 all-gather.2
  231.3 251.8 all-reduce.1
where the time goes:
time: 495 us; the launch traced here: 493 us
  waiting for transfers between devices  401 us (81%)
  other arithmetic  47 us (9%)
  local copies, waits for them, and re-layouts  16.6 us (3%)
  starting transfers between devices  13.6 us (3%)
  between operations  13.6 us (3%)
    psum x1, waiting for transfers between devices, per_device(): summed = lax.psum(contribution, 'gz')  252 us
    all_gather x1, waiting for transfers between devices, carried_in(): everything = lax.all_gather(array, axis)  141 us
    select_n x32, other arithmetic, step(): return jnp.where(reached, new, before)  27.5 us
    mul x1, other arithmetic, shade_block(): weighted = shading * opacity  13.9 us
  transfers between devices with their start and end apart: 8, of which 6 were waited for; matrix products, arithmetic and copies ran while one was open for 2% of the time, Pallas kernels for 0%

commit v1 on v0

v1 whole, which is shorter than its diff:
```python
import functools

import jax
import jax.numpy as jnp
from jax import lax
from jax.experimental import pallas as pl
from jax.experimental.pallas import tpu as pltpu
from jax.sharding import PartitionSpec as P

LOG2E = 1.4426950408889634
E = 2.718281828459045
VMEM = pltpu.VMEM


def whole():
    return pl.BlockSpec(memory_space=VMEM)


def faces_kernel(v_ref, zlo_ref, zhi_ref, xlo_ref, xhi_ref, y_ref):
    nz, nx, ny = v_ref.shape
    zlo_ref[...] = v_ref[0]
    zhi_ref[...] = v_ref[nz - 1]
    for z in range(nz):
        xlo_ref[z : z + 1, :] = v_ref[z, 0:1, :]
        xhi_ref[z : z + 1, :] = v_ref[z, nx - 1 : nx, :]
    lane_pair = lax.broadcasted_iota(jnp.int32, (8, ny), 1) // 2

    @pl.loop(0, nx // 8)
    def _(j):
        rows = pl.ds(pl.multiple_of(j * 8, 8), 8)
        packed = jnp.zeros((8, ny), jnp.float32)
        for z in range(nz):
            turned = pltpu.roll(v_ref[z, rows, :], 2 * z + 1, 1)
            packed = jnp.where(lane_pair == z, turned, packed)
        y_ref[rows, :] = packed


def faces(volume):
    nz, nx, ny = volume.shape
    plane = jax.ShapeDtypeStruct((nx, ny), jnp.float32)
    row = jax.ShapeDtypeStruct((nz, ny), jnp.float32)
    return pl.pallas_call(
        faces_kernel,
        out_shape=(plane, plane, row, row, plane),
        in_specs=[whole()],
        out_specs=[whole()] * 5,
        compiler_params=pltpu.CompilerParams(vmem_limit_bytes=8 << 20),
        cost_estimate=pl.CostEstimate(flops=1 << 20, bytes_accessed=nz * nx * ny * 4, transcendentals=0),
        name="faces",
    )(volume)


def render_kernel(scale, v_ref, zlo_ref, zhi_ref, xlo_ref, xhi_ref, ylo_ref, yhi_ref, out_ref, grid_ref, edge_ref, part_ref, sem):
    nz, nx, ny = v_ref.shape
    copy = pltpu.make_async_copy(v_ref, grid_ref.at[1 : nz + 1, 8 : nx + 8, :], sem)
    copy.start()
    lane = lax.broadcasted_iota(jnp.int32, (nx, ny), 1)
    edge_ref[...] = jnp.where(lane % 2 == 1, pltpu.roll(ylo_ref[...], 1, 1), pltpu.roll(yhi_ref[...], ny - 1, 1))
    grid_ref[0, 8 : nx + 8, :] = zlo_ref[...]
    grid_ref[nz + 1, 8 : nx + 8, :] = zhi_ref[...]
    for z in range(nz):
        grid_ref[z + 1, 7:8, :] = xlo_ref[z : z + 1, :]
        grid_ref[z + 1, nx + 8 : nx + 9, :] = xhi_ref[z : z + 1, :]
    copy.wait()
    height = 16
    col = lax.broadcasted_iota(jnp.int32, (height, ny), 1)
    first, last = col == 0, col == ny - 1

    for block in range(nx // height):
        start = block * height
        edge = edge_ref[start : start + height, :]

        def step(z, carry):
            prev, cur, clear, red, green, blue = carry
            new = grid_ref[z + 2, start + 8 : start + 8 + height, :]
            above = grid_ref[z + 1, start + 7 : start + 7 + height, :]
            below = grid_ref[z + 1, start + 9 : start + 9 + height, :]
            outer = pltpu.roll(edge, ny - 1 - 2 * z, 1)
            left = jnp.where(first, outer, pltpu.roll(cur, 1, 1))
            right = jnp.where(last, outer, pltpu.roll(cur, ny - 1, 1))
            dz = new - prev
            dx = below - above
            dy = right - left
            facing = jnp.abs(2.0 * (dz + dy) + dx)
            shading = 0.2 + (2.0 / 3.0) * facing * lax.rsqrt(dz * dz + dx * dx + dy * dy + 4.0)
            grown = jnp.exp(cur)
            thick = grown * scale
            opacity = thick * (1.0 + thick * (-1.0 / 2 + thick * (1.0 / 6 + thick * (-1.0 / 24 + thick * (1.0 / 120)))))
            square = grown * grown
            up = square * E
            low = 1.0 + square * (1.0 / E)
            ratio = 1.0 / ((1.0 + up) * low)
            weight = clear * opacity
            lit = weight * shading
            red = red + lit * (up * low * ratio)
            green = green + lit * jnp.exp(-cur * cur)
            blue = blue + lit * ((1.0 + up) * ratio)
            return (cur, new, clear - weight, red, green, blue)

        zero = jnp.zeros((height, ny), jnp.float32)
        carry = (
            grid_ref[0, start + 8 : start + 8 + height, :],
            grid_ref[1, start + 8 : start + 8 + height, :],
            zero + 1.0,
            zero,
            zero,
            zero,
        )
        carry = lax.fori_loop(0, nz, step, carry, unroll=4)
        _, _, clear, red, green, blue = carry
        for c, value in enumerate((red, green, blue, clear)):
            part_ref[c, start : start + height, :] = value
    chunk = out_ref.shape[1] // 4
    for k in range(out_ref.shape[0]):
        for c in range(4):
            out_ref[k, c * chunk : (c + 1) * chunk, :] = part_ref[c, k * chunk : (k + 1) * chunk, :]


def render(volume, halo, depth_cells, pieces):
    nz, nx, ny = volume.shape
    return pl.pallas_call(
        functools.partial(render_kernel, 2.0 / depth_cells),
        out_shape=jax.ShapeDtypeStruct((pieces, 4 * nx // pieces, ny), jnp.float32),
        in_specs=[pl.BlockSpec(memory_space=pl.ANY)] + [whole()] * 6,
        out_specs=whole(),
        scratch_shapes=[
            VMEM((nz + 2, nx + 16, ny), jnp.float32),
            VMEM((nx, ny), jnp.float32),
            VMEM((4, nx, ny), jnp.float32),
            pltpu.SemaphoreType.DMA,
        ],
        compiler_params=pltpu.CompilerParams(vmem_limit_bytes=16 << 20),
        name="render",
    )(volume, *halo)


def merge_kernel(parts_ref, out_ref):
    count, rows, ny = parts_ref.shape
    part = rows // 4
    shape = (part, ny)
    clear = jnp.ones(shape, jnp.float32)
    total = [jnp.zeros(shape, jnp.float32) for _ in range(3)]
    for k in range(count):
        for c in range(3):
            total[c] = total[c] + clear * parts_ref[k, c * part : (c + 1) * part, :]
        clear = clear * parts_ref[k, 3 * part :, :]
    total.append(1.0 - clear)
    for k in range(out_ref.shape[0]):
        for c in range(4):
            out_ref[k, c * part : (c + 1) * part, :] = total[c]


def merge(parts, copies):
    _, rows, ny = parts.shape
    return pl.pallas_call(
        merge_kernel,
        out_shape=jax.ShapeDtypeStruct((copies, rows, ny), jnp.float32),
        in_specs=[whole()],
        out_specs=whole(),
        compiler_params=pltpu.CompilerParams(vmem_limit_bytes=8 << 20),
        name="merge",
    )(parts)


def lay_kernel(parts_ref, out_ref):
    count, rows, ny = parts_ref.shape
    part = rows // 4
    for k in range(count):
        for c in range(4):
            out_ref[c, k * part : (k + 1) * part, :] = parts_ref[k, c * part : (c + 1) * part, :]


def lay(parts):
    count, rows, ny = parts.shape
    return pl.pallas_call(
        lay_kernel,
        out_shape=jax.ShapeDtypeStruct((4, count * rows // 4, ny), jnp.float32),
        in_specs=[whole()],
        out_specs=whole(),
        compiler_params=pltpu.CompilerParams(vmem_limit_bytes=8 << 20),
        name="lay",
    )(parts)


def shift(array, axis, upward):
    devices = lax.axis_size(axis)
    pairs = [(i, i + 1) if upward else (i + 1, i) for i in range(devices - 1)]
    return lax.ppermute(array, axis, pairs)


def per_device(volume):
    bricks = lax.axis_size("gz")
    depth_cells = volume.shape[0] * bricks
    zlo, zhi, xlo, xhi, y = faces(volume)
    halo = (
        shift(zhi, "gz", True),
        shift(zlo, "gz", False),
        shift(xhi, "gx", True),
        shift(xlo, "gx", False),
        shift(y, "gy", True),
        shift(y, "gy", False),
    )
    parts = render(volume, halo, depth_cells, bricks)
    parts = lax.all_to_all(parts, "gz", 0, 0)
    merged = merge(parts, bricks)
    return lay(lax.all_to_all(merged, "gz", 0, 0))


def solution(mesh):
    return jax.shard_map(
        per_device,
        mesh=mesh,
        in_specs=(P("gz", "gx", "gy"),),
        out_specs=P(None, "gx", "gy"),
        check_vma=False,
    )
```

time: 495 us -> 149 us (0.30)
  waiting for transfers between devices: 401 us -> 5.77 us
  blocking collectives: 0 us -> 117 us
  other arithmetic: 47 us -> 0 us
  local copies, waits for them, and re-layouts: 16.6 us -> 1.59 us
  between operations: 13.6 us -> 0.09 us
  Pallas kernels: 0 us -> 9.79 us
    psum x1 -> x0, waiting for transfers between devices: 252 us -> none  [per_device(): summed = lax.psum(contribution, 'gz')]
    all_gather x1 -> x0, waiting for transfers between devices: 141 us -> none  [carried_in(): everything = lax.all_gather(array, axis)]
    all_to_all x0 -> x2, blocking collectives: none -> 117 us  [the longest x1 72.5 us: per_device(): parts = lax.all_to_all(parts, 'gz', 0, 0)]
    select_n x32 -> x0, other arithmetic: 27.5 us -> none  [step(): return jnp.where(reached, new, before)]
    mul x3 -> x0, other arithmetic: 13.9 us -> none  [the longest x1 13.9 us: shade_block(): weighted = shading * opacity]
    pallas_call x0 -> x4, Pallas kernels: none -> 9.79 us  [the longest x1 7.32 us: render(): pl.pallas_call(functools.partial(render_kernel, 2.0 / depth_cells), out_s...]
    slice x6 -> x0, local copies, waits for them, and re-layouts: 8.22 us -> none  [the longest x3 5.98 us: with_halo(): initial = lax.slice_in_dim(array, 0, width, axis=dim)]
  transfers between devices with their start and end apart: 8 -> 6, of which waited for: 6 -> 2; matrix products, arithmetic and copies ran while one was open for 2% -> 0% of each run, Pallas kernels for 0% -> 0%
where the time goes in v1:
time: 149 us; the launch traced here: 147 us
  blocking collectives  117 us (79%)
  starting transfers between devices  13.5 us (9%)
  Pallas kernels  9.79 us (7%)
  waiting for transfers between devices  5.77 us (4%)
  local copies, waits for them, and re-layouts  1.59 us (1%)
    all_to_all x1, blocking collectives, per_device(): parts = lax.all_to_all(parts, 'gz', 0, 0)  72.5 us
    all_to_all x1, blocking collectives, per_device(): return lay(lax.all_to_all(merged, 'gz', 0, 0))  44.2 us
    ppermute x6, starting transfers between devices, shift(): return lax.ppermute(array, axis, pairs)  13.5 us
    pallas_call x1, Pallas kernels, render(): pl.pallas_call(functools.partial(render_kernel, 2.0 / depth_cells), out_s...  7.32 us
    ppermute x6, waiting for transfers between devices, shift(): return lax.ppermute(array, axis, pairs)  5.77 us
  transfers between devices with their start and end apart: 6, of which 2 were waited for; matrix products, arithmetic and copies ran while one was open for 0% of the time, Pallas kernels for 0%

profile of v1, /device:TPU:6, one launch (start us, length us, event | category | flops | bytes accessed | tf_op | source)
XLA Modules:
  0.0 147.4 jit_solution(1498185848435732136)
XLA Ops:
  0.0 0.0 copy-start
  0.0 1.6 %copy-done = f32[32,128,128]{2,1,0:T(8,128)S(1)} copy-done((f32[32,128,128]{2,1,0:T(8,128)S(1)}, f32[32,128,128]{2,1,0:T(8,128)}, u32[]{:S(2)}) %copy-start) | copy-done | bytes 2097176
  1.6 0.0 copy-start.1
  1.6 1.7 %faces.1 = (f32[128,128]{1,0:T(8,128)S(1)}, f32[128,128]{1,0:T(8,128)S(1)}, f32[32,128]{1,0:T(8,128)S(1)}, f32[32,128]{1,0:T(8,128)S(1)}, f32[128,128]{1,0:T(8,128)S(1)}) custom-call(f32[32,128,128]{2,1,0:T(8,128)S(1)} %copy-done), custom_call_target="tpu_custom_call" | custom-call | flops 1048576 | bytes 2097152 | tf_op jit(solution)/shard_map/faces/pallas_call | solution.py:42
  3.3 3.8 %collective-permute-start = (f32[128,128]{1,0:T(8,128)S(1)}, f32[128,128]{1,0:T(8,128)S(1)}, u32[]{:S(2)}, u32[]{:S(2)}) collective-permute-start(f32[128,128]{1,0:T(8,128)S(1)} %get-tuple-element.10), channel_id=1, source_target_pairs={{0,1},{1,2},{2,3},{3,4},{4,5},{5,6},{6,7},{7,8},{8,9},{9,10},{10,1... | collective-permute-start | bytes 196616 | tf_op jit(solution)/shard_map/ppermute | solution.py:188
  7.1 1.3 collective-permute-start.1
  8.4 1.3 collective-permute-start.5
  9.7 3.0 %collective-permute-start.4 = (f32[128,128]{1,0:T(8,128)S(1)}, f32[128,128]{1,0:T(8,128)S(1)}, u32[]{:S(2)}, u32[]{:S(2)}) collective-permute-start(f32[128,128]{1,0:T(8,128)S(1)} %get-tuple-element.14), channel_id=1, source_target_pairs={{0,32},{32,64},{64,96},{96,128},{128,160},{160,192},{192,224},{1,3... | collective-permute-start | bytes 196616 | tf_op jit(solution)/shard_map/ppermute | solution.py:188
  12.7 1.3 collective-permute-start.2
  14.0 4.3 %collective-permute-done.2.xlo_ref = f32[32,128]{1,0:T(8,128)S(1)} collective-permute-done((f32[32,128]{1,0:T(8,128)S(1)}, f32[32,128]{1,0:T(8,128)S(1)}, u32[]{:S(2)}, u32[]{:S(2)}) %collective-permute-start.2) | collective-permute-done | bytes 16416 | tf_op jit(solution)/shard_map/ppermute | solution.py:188
  18.4 2.7 %collective-permute-start.3 = (f32[32,128]{1,0:T(8,128)S(1)}, f32[32,128]{1,0:T(8,128)S(1)}, u32[]{:S(2)}, u32[]{:S(2)}) collective-permute-start(f32[32,128]{1,0:T(8,128)S(1)} %get-tuple-element.13), channel_id=1, source_target_pairs={{256,0},{512,256},{768,512},{257,1},{513,257},{769,513},{258,2},{5... | collective-permute-start | bytes 49160 | tf_op jit(solution)/shard_map/ppermute | solution.py:188
  21.1 1.4 collective-permute-done.3.xhi_ref
  22.5 0.0 collective-permute-done.zlo_ref
  22.5 0.0 collective-permute-done.1.zhi_ref
  22.5 0.0 collective-permute-done.5.yhi_ref
  22.5 0.0 collective-permute-done.4.ylo_ref
  22.5 0.0 copy-done.1
  22.6 7.3 %render.1 = f32[32,16,128]{2,1,0:T(8,128)S(1)} custom-call(f32[32,128,128]{2,1,0:T(8,128)S(1)} %copy-done.1, f32[128,128]{1,0:T(8,128)S(1)} %collective-permute-done.zlo_ref, f32[128,128]{1,0:T(8,128)S(1)} %collective-permute-done.1.zhi_ref, f32[32,128]{1,0:T(8,128)S(1)} %collective-permute-done.2.xlo_ref, f32[32,128]{1,0:T(8,128)S(1)} %collective-permute-done.3.xhi_ref, ...), custom_call_target="tpu_custom_call" | custom-call | tf_op jit(solution)/shard_map/render/pallas_call | solution.py:121
  29.9 72.5 %all_to_all.10.parts_ref = f32[32,16,128]{2,1,0:T(8,128)S(1)} all-to-all(f32[32,16,128]{2,1,0:T(8,128)S(1)} %render.1), channel_id=1, replica_groups=mesh['gx'=4,'gy'=8,'gz'=32] {'gz'}, dimensions={0} | all-to-all | bytes 524288 | tf_op jit(solution)/shard_map/all_to_all | solution.py:204
  102.4 0.1 merge.1
  102.5 44.2 %all_to_all.11.parts_ref = f32[32,16,128]{2,1,0:T(8,128)S(1)} all-to-all(f32[32,16,128]{2,1,0:T(8,128)S(1)} %merge.1), channel_id=1, replica_groups=mesh['gx'=4,'gy'=8,'gz'=32] {'gz'}, dimensions={0} | all-to-all | bytes 524288 | tf_op jit(solution)/shard_map/all_to_all | solution.py:206
  146.7 0.7 lay.1
Async XLA Ops:
  0.0 1.6 %copy-start = (f32[32,128,128]{2,1,0:T(8,128)S(1)}, f32[32,128,128]{2,1,0:T(8,128)}, u32[]{:S(2)}) copy-start(f32[32,128,128]{2,1,0:T(8,128)} %v_ref.3) | copy-start | bytes 6291460
  1.6 21.0 %copy-start.1 = (f32[32,128,128]{2,1,0:T(8,128)S(1)}, f32[32,128,128]{2,1,0:T(8,128)}, u32[]{:S(2)}) copy-start(f32[32,128,128]{2,1,0:T(8,128)} %v_ref.3) | copy-start | bytes 6291460
  3.3 19.3 %collective-permute-start = (f32[128,128]{1,0:T(8,128)S(1)}, f32[128,128]{1,0:T(8,128)S(1)}, u32[]{:S(2)}, u32[]{:S(2)}) collective-permute-start(f32[128,128]{1,0:T(8,128)S(1)} %get-tuple-element.10), channel_id=1, source_target_pairs={{0,1},{1,2},{2,3},{3,4},{4,5},{5,6},{6,7},{7,8},{8,9},{9,10},{10,1... | collective-permute-start | bytes 196616 | tf_op jit(solution)/shard_map/ppermute | solution.py:188
  7.1 15.4 %collective-permute-start.1 = (f32[128,128]{1,0:T(8,128)S(1)}, f32[128,128]{1,0:T(8,128)S(1)}, u32[]{:S(2)}, u32[]{:S(2)}) collective-permute-start(f32[128,128]{1,0:T(8,128)S(1)} %get-tuple-element.11), channel_id=1, source_target_pairs={{1,0},{2,1},{3,2},{4,3},{5,4},{6,5},{7,6},{8,7},{9,8},{10,9},{11,1... | collective-permute-start | bytes 196616 | tf_op jit(solution)/shard_map/ppermute | solution.py:188
  8.4 14.1 %collective-permute-start.5 = (f32[128,128]{1,0:T(8,128)S(1)}, f32[128,128]{1,0:T(8,128)S(1)}, u32[]{:S(2)}, u32[]{:S(2)}) collective-permute-start(f32[128,128]{1,0:T(8,128)S(1)} %get-tuple-element.14), channel_id=1, source_target_pairs={{32,0},{64,32},{96,64},{128,96},{160,128},{192,160},{224,192},{33,... | collective-permute-start | bytes 196616 | tf_op jit(solution)/shard_map/ppermute | solution.py:188
  9.7 12.8 %collective-permute-start.4 = (f32[128,128]{1,0:T(8,128)S(1)}, f32[128,128]{1,0:T(8,128)S(1)}, u32[]{:S(2)}, u32[]{:S(2)}) collective-permute-start(f32[128,128]{1,0:T(8,128)S(1)} %get-tuple-element.14), channel_id=1, source_target_pairs={{0,32},{32,64},{64,96},{96,128},{128,160},{160,192},{192,224},{1,3... | collective-permute-start | bytes 196616 | tf_op jit(solution)/shard_map/ppermute | solution.py:188
  12.7 5.6 %collective-permute-start.2 = (f32[32,128]{1,0:T(8,128)S(1)}, f32[32,128]{1,0:T(8,128)S(1)}, u32[]{:S(2)}, u32[]{:S(2)}) collective-permute-start(f32[32,128]{1,0:T(8,128)S(1)} %get-tuple-element.12), channel_id=1, source_target_pairs={{0,256},{256,512},{512,768},{1,257},{257,513},{513,769},{2,258},{2... | collective-permute-start | bytes 49160 | tf_op jit(solution)/shard_map/ppermute | solution.py:188
  18.4 4.2 %collective-permute-start.3 = (f32[32,128]{1,0:T(8,128)S(1)}, f32[32,128]{1,0:T(8,128)S(1)}, u32[]{:S(2)}, u32[]{:S(2)}) collective-permute-start(f32[32,128]{1,0:T(8,128)S(1)} %get-tuple-element.13), channel_id=1, source_target_pairs={{256,0},{512,256},{768,512},{257,1},{513,257},{769,513},{258,2},{5... | collective-permute-start | bytes 49160 | tf_op jit(solution)/shard_map/ppermute | solution.py:188

commit v2 on v1

--- a/solution.py
+++ b/solution.py
@@ -50,7 +50,7 @@
     )(volume)
 
 
-def render_kernel(scale, v_ref, zlo_ref, zhi_ref, xlo_ref, xhi_ref, ylo_ref, yhi_ref, out_ref, grid_ref, edge_ref, part_ref, sem):
+def render_kernel(scale, v_ref, zlo_ref, zhi_ref, xlo_ref, xhi_ref, ylo_ref, yhi_ref, out_ref, grid_ref, edge_ref, sem):
     nz, nx, ny = v_ref.shape
     copy = pltpu.make_async_copy(v_ref, grid_ref.at[1 : nz + 1, 8 : nx + 8, :], sem)
     copy.start()
@@ -62,7 +62,7 @@
         grid_ref[z + 1, 7:8, :] = xlo_ref[z : z + 1, :]
         grid_ref[z + 1, nx + 8 : nx + 9, :] = xhi_ref[z : z + 1, :]
     copy.wait()
-    height = 16
+    height = nx // out_ref.shape[0]
     col = lax.broadcasted_iota(jnp.int32, (height, ny), 1)
     first, last = col == 0, col == ny - 1
 
@@ -109,11 +109,7 @@
         carry = lax.fori_loop(0, nz, step, carry, unroll=4)
         _, _, clear, red, green, blue = carry
         for c, value in enumerate((red, green, blue, clear)):
-            part_ref[c, start : start + height, :] = value
-    chunk = out_ref.shape[1] // 4
-    for k in range(out_ref.shape[0]):
-        for c in range(4):
-            out_ref[k, c * chunk : (c + 1) * chunk, :] = part_ref[c, k * chunk : (k + 1) * chunk, :]
+            out_ref[block, c * height : (c + 1) * height, :] = value
 
 
 def render(volume, halo, depth_cells, pieces):
@@ -126,7 +122,6 @@
         scratch_shapes=[
             VMEM((nz + 2, nx + 16, ny), jnp.float32),
             VMEM((nx, ny), jnp.float32),
-            VMEM((4, nx, ny), jnp.float32),
             pltpu.SemaphoreType.DMA,
         ],
         compiler_params=pltpu.CompilerParams(vmem_limit_bytes=16 << 20),
@@ -134,26 +129,25 @@
     )(volume, *halo)
 
 
-def merge_kernel(parts_ref, out_ref):
+def merge_kernel(final, parts_ref, out_ref):
     count, rows, ny = parts_ref.shape
     part = rows // 4
-    shape = (part, ny)
-    clear = jnp.ones(shape, jnp.float32)
-    total = [jnp.zeros(shape, jnp.float32) for _ in range(3)]
-    for k in range(count):
+    clear = parts_ref[0, 3 * part :, :]
+    total = [parts_ref[0, c * part : (c + 1) * part, :] for c in range(3)]
+    for k in range(1, count):
         for c in range(3):
             total[c] = total[c] + clear * parts_ref[k, c * part : (c + 1) * part, :]
         clear = clear * parts_ref[k, 3 * part :, :]
-    total.append(1.0 - clear)
+    total.append(1.0 - clear if final else clear)
     for k in range(out_ref.shape[0]):
         for c in range(4):
             out_ref[k, c * part : (c + 1) * part, :] = total[c]
 
 
-def merge(parts, copies):
+def merge(parts, copies, final):
     _, rows, ny = parts.shape
     return pl.pallas_call(
-        merge_kernel,
+        functools.partial(merge_kernel, final),
         out_shape=jax.ShapeDtypeStruct((copies, rows, ny), jnp.float32),
         in_specs=[whole()],
         out_specs=whole(),
@@ -200,10 +194,16 @@
         shift(y, "gy", True),
         shift(y, "gy", False),
     )
-    parts = render(volume, halo, depth_cells, bricks)
-    parts = lax.all_to_all(parts, "gz", 0, 0)
-    merged = merge(parts, bricks)
-    return lay(lax.all_to_all(merged, "gz", 0, 0))
+    near = max(n for n in (1, 2, 4, 8) if bricks % n == 0)
+    far = bricks // near
+    runs = [[g * near + i for i in range(near)] for g in range(far)]
+    strides = [[g * near + i for g in range(far)] for i in range(near)]
+    parts = render(volume, halo, depth_cells, near)
+    parts = lax.all_to_all(parts, "gz", 0, 0, axis_index_groups=runs)
+    parts = merge(parts, far, False)
+    parts = lax.all_to_all(parts, "gz", 0, 0, axis_index_groups=strides)
+    parts = merge(parts, near, True)
+    return lay(lax.all_to_all(parts, "gz", 0, 0, axis_index_groups=runs))
 
 
 def solution(mesh):

time: 149 us -> 129 us (0.87)
  blocking collectives: 117 us -> 96.5 us
    all_to_all x2 -> x3, blocking collectives: 117 us -> 96.5 us  [the longest x1 45.2 us: per_device(): parts = lax.all_to_all(parts, 'gz', 0, 0, axis_index_groups=strides)]
where the time goes in v2:
time: 129 us; the launch traced here: 127 us
  blocking collectives  96.5 us (75%)
  starting transfers between devices  13.5 us (10%)
  Pallas kernels  9.72 us (8%)
  waiting for transfers between devices  5.77 us (4%)
  local copies, waits for them, and re-layouts  1.59 us (1%)
    all_to_all x1, blocking collectives, per_device(): parts = lax.all_to_all(parts, 'gz', 0, 0, axis_index_groups=strides)  45.2 us
    all_to_all x1, blocking collectives, per_device(): parts = lax.all_to_all(parts, 'gz', 0, 0, axis_index_groups=runs)  30.3 us
    all_to_all x1, blocking collectives, per_device(): return lay(lax.all_to_all(parts, 'gz', 0, 0, axis_index_groups=runs))  21 us
    ppermute x6, starting transfers between devices, shift(): return lax.ppermute(array, axis, pairs)  13.5 us
    pallas_call x1, Pallas kernels, render(): pl.pallas_call(functools.partial(render_kernel, 2.0 / depth_cells), out_s...  7.3 us
    ppermute x6, waiting for transfers between devices, shift(): return lax.ppermute(array, axis, pairs)  5.77 us
  transfers between devices with their start and end apart: 6, of which 2 were waited for; matrix products, arithmetic and copies ran while one was open for 0% of the time, Pallas kernels for 0%

profile of v2, /device:TPU:6, one launch (start us, length us, event | category | flops | bytes accessed | tf_op | source)
XLA Modules:
  0.0 127.1 jit_solution(7932218910007076923)
XLA Ops:
  0.0 0.0 copy-start
  0.0 1.6 %copy-done = f32[32,128,128]{2,1,0:T(8,128)S(1)} copy-done((f32[32,128,128]{2,1,0:T(8,128)S(1)}, f32[32,128,128]{2,1,0:T(8,128)}, u32[]{:S(2)}) %copy-start) | copy-done | bytes 2097176
  1.6 0.0 copy-start.1
  1.6 1.7 %faces.1 = (f32[128,128]{1,0:T(8,128)S(1)}, f32[128,128]{1,0:T(8,128)S(1)}, f32[32,128]{1,0:T(8,128)S(1)}, f32[32,128]{1,0:T(8,128)S(1)}, f32[128,128]{1,0:T(8,128)S(1)}) custom-call(f32[32,128,128]{2,1,0:T(8,128)S(1)} %copy-done), custom_call_target="tpu_custom_call" | custom-call | flops 1048576 | bytes 2097152 | tf_op jit(solution)/shard_map/faces/pallas_call | solution.py:42
  3.3 3.8 %collective-permute-start = (f32[128,128]{1,0:T(8,128)S(1)}, f32[128,128]{1,0:T(8,128)S(1)}, u32[]{:S(2)}, u32[]{:S(2)}) collective-permute-start(f32[128,128]{1,0:T(8,128)S(1)} %get-tuple-element.10), channel_id=1, source_target_pairs={{0,1},{1,2},{2,3},{3,4},{4,5},{5,6},{6,7},{7,8},{8,9},{9,10},{10,1... | collective-permute-start | bytes 196616 | tf_op jit(solution)/shard_map/ppermute | solution.py:182
  7.1 1.3 %collective-permute-start.1 = (f32[128,128]{1,0:T(8,128)S(1)}, f32[128,128]{1,0:T(8,128)S(1)}, u32[]{:S(2)}, u32[]{:S(2)}) collective-permute-start(f32[128,128]{1,0:T(8,128)S(1)} %get-tuple-element.11), channel_id=1, source_target_pairs={{1,0},{2,1},{3,2},{4,3},{5,4},{6,5},{7,6},{8,7},{9,8},{10,9},{11,1... | collective-permute-start | bytes 196616 | tf_op jit(solution)/shard_map/ppermute | solution.py:182
  8.4 1.3 %collective-permute-start.5 = (f32[128,128]{1,0:T(8,128)S(1)}, f32[128,128]{1,0:T(8,128)S(1)}, u32[]{:S(2)}, u32[]{:S(2)}) collective-permute-start(f32[128,128]{1,0:T(8,128)S(1)} %get-tuple-element.14), channel_id=1, source_target_pairs={{32,0},{64,32},{96,64},{128,96},{160,128},{192,160},{224,192},{33,... | collective-permute-start | bytes 196616 | tf_op jit(solution)/shard_map/ppermute | solution.py:182
  9.7 3.0 %collective-permute-start.4 = (f32[128,128]{1,0:T(8,128)S(1)}, f32[128,128]{1,0:T(8,128)S(1)}, u32[]{:S(2)}, u32[]{:S(2)}) collective-permute-start(f32[128,128]{1,0:T(8,128)S(1)} %get-tuple-element.14), channel_id=1, source_target_pairs={{0,32},{32,64},{64,96},{96,128},{128,160},{160,192},{192,224},{1,3... | collective-permute-start | bytes 196616 | tf_op jit(solution)/shard_map/ppermute | solution.py:182
  12.7 1.3 %collective-permute-start.2 = (f32[32,128]{1,0:T(8,128)S(1)}, f32[32,128]{1,0:T(8,128)S(1)}, u32[]{:S(2)}, u32[]{:S(2)}) collective-permute-start(f32[32,128]{1,0:T(8,128)S(1)} %get-tuple-element.12), channel_id=1, source_target_pairs={{0,256},{256,512},{512,768},{1,257},{257,513},{513,769},{2,258},{2... | collective-permute-start | bytes 49160 | tf_op jit(solution)/shard_map/ppermute | solution.py:182
  14.0 4.3 %collective-permute-done.2.xlo_ref = f32[32,128]{1,0:T(8,128)S(1)} collective-permute-done((f32[32,128]{1,0:T(8,128)S(1)}, f32[32,128]{1,0:T(8,128)S(1)}, u32[]{:S(2)}, u32[]{:S(2)}) %collective-permute-start.2) | collective-permute-done | bytes 16416 | tf_op jit(solution)/shard_map/ppermute | solution.py:182
  18.4 2.7 %collective-permute-start.3 = (f32[32,128]{1,0:T(8,128)S(1)}, f32[32,128]{1,0:T(8,128)S(1)}, u32[]{:S(2)}, u32[]{:S(2)}) collective-permute-start(f32[32,128]{1,0:T(8,128)S(1)} %get-tuple-element.13), channel_id=1, source_target_pairs={{256,0},{512,256},{768,512},{257,1},{513,257},{769,513},{258,2},{5... | collective-permute-start | bytes 49160 | tf_op jit(solution)/shard_map/ppermute | solution.py:182
  21.1 1.4 %collective-permute-done.3.xhi_ref = f32[32,128]{1,0:T(8,128)S(1)} collective-permute-done((f32[32,128]{1,0:T(8,128)S(1)}, f32[32,128]{1,0:T(8,128)S(1)}, u32[]{:S(2)}, u32[]{:S(2)}) %collective-permute-start.3) | collective-permute-done | bytes 16416 | tf_op jit(solution)/shard_map/ppermute | solution.py:182
  22.5 0.0 collective-permute-done.zlo_ref
  22.5 0.0 collective-permute-done.1.zhi_ref
  22.5 0.0 collective-permute-done.5.yhi_ref
  22.5 0.0 collective-permute-done.4.ylo_ref
  22.5 0.0 copy-done.1
  22.6 7.3 %render.1 = f32[8,64,128]{2,1,0:T(8,128)S(1)} custom-call(f32[32,128,128]{2,1,0:T(8,128)S(1)} %copy-done.1, f32[128,128]{1,0:T(8,128)S(1)} %collective-permute-done.zlo_ref, f32[128,128]{1,0:T(8,128)S(1)} %collective-permute-done.1.zhi_ref, f32[32,128]{1,0:T(8,128)S(1)} %collective-permute-done.2.xlo_ref, f32[32,128]{1,0:T(8,128)S(1)} %collective-permute-done.3.xhi_ref, ...), custom_call_target="tpu_custom_call" | custom-call | tf_op jit(solution)/shard_map/render/pallas_call | solution.py:117
  29.9 30.3 %all_to_all.15.parts_ref = f32[8,64,128]{2,1,0:T(8,128)S(1)} all-to-all(f32[8,64,128]{2,1,0:T(8,128)S(1)} %render.1), channel_id=1, replica_groups={{0,1,2,3,4,5,6,7},{8,9,10,11,12,13,14,15},{16,17,18,19,20,21,22,23},{24..., dimensions={0} | all-to-all | bytes 524288 | tf_op jit(solution)/shard_map/all_to_all | solution.py:202
  60.2 45.2 %all_to_all.16.parts_ref = f32[4,64,128]{2,1,0:T(8,128)S(1)} all-to-all(f32[4,64,128]{2,1,0:T(8,128)S(1)} %merge.2), channel_id=1, replica_groups={{0,8,16,24},{1,9,17,25},{2,10,18,26},{3,11,19,27},{4,12,20,28},{5,13,21..., dimensions={0} | all-to-all | bytes 262144 | tf_op jit(solution)/shard_map/all_to_all | solution.py:204
  105.4 21.0 %all_to_all.17.parts_ref = f32[8,64,128]{2,1,0:T(8,128)S(1)} all-to-all(f32[8,64,128]{2,1,0:T(8,128)S(1)} %merge.3), channel_id=1, replica_groups={{0,1,2,3,4,5,6,7},{8,9,10,11,12,13,14,15},{16,17,18,19,20,21,22,23},{24..., dimensions={0} | all-to-all | bytes 524288 | tf_op jit(solution)/shard_map/all_to_all | solution.py:206
  126.4 0.7 lay.1
  (2 shorter events, 0.0 us)
Async XLA Ops:
  0.0 1.6 %copy-start = (f32[32,128,128]{2,1,0:T(8,128)S(1)}, f32[32,128,128]{2,1,0:T(8,128)}, u32[]{:S(2)}) copy-start(f32[32,128,128]{2,1,0:T(8,128)} %v_ref.3) | copy-start | bytes 6291460
  1.6 21.0 %copy-start.1 = (f32[32,128,128]{2,1,0:T(8,128)S(1)}, f32[32,128,128]{2,1,0:T(8,128)}, u32[]{:S(2)}) copy-start(f32[32,128,128]{2,1,0:T(8,128)} %v_ref.3) | copy-start | bytes 6291460
  3.3 19.3 %collective-permute-start = (f32[128,128]{1,0:T(8,128)S(1)}, f32[128,128]{1,0:T(8,128)S(1)}, u32[]{:S(2)}, u32[]{:S(2)}) collective-permute-start(f32[128,128]{1,0:T(8,128)S(1)} %get-tuple-element.10), channel_id=1, source_target_pairs={{0,1},{1,2},{2,3},{3,4},{4,5},{5,6},{6,7},{7,8},{8,9},{9,10},{10,1... | collective-permute-start | bytes 196616 | tf_op jit(solution)/shard_map/ppermute | solution.py:182
  7.1 15.4 %collective-permute-start.1 = (f32[128,128]{1,0:T(8,128)S(1)}, f32[128,128]{1,0:T(8,128)S(1)}, u32[]{:S(2)}, u32[]{:S(2)}) collective-permute-start(f32[128,128]{1,0:T(8,128)S(1)} %get-tuple-element.11), channel_id=1, source_target_pairs={{1,0},{2,1},{3,2},{4,3},{5,4},{6,5},{7,6},{8,7},{9,8},{10,9},{11,1... | collective-permute-start | bytes 196616 | tf_op jit(solution)/shard_map/ppermute | solution.py:182
  8.4 14.1 %collective-permute-start.5 = (f32[128,128]{1,0:T(8,128)S(1)}, f32[128,128]{1,0:T(8,128)S(1)}, u32[]{:S(2)}, u32[]{:S(2)}) collective-permute-start(f32[128,128]{1,0:T(8,128)S(1)} %get-tuple-element.14), channel_id=1, source_target_pairs={{32,0},{64,32},{96,64},{128,96},{160,128},{192,160},{224,192},{33,... | collective-permute-start | bytes 196616 | tf_op jit(solution)/shard_map/ppermute | solution.py:182
  9.7 12.8 %collective-permute-start.4 = (f32[128,128]{1,0:T(8,128)S(1)}, f32[128,128]{1,0:T(8,128)S(1)}, u32[]{:S(2)}, u32[]{:S(2)}) collective-permute-start(f32[128,128]{1,0:T(8,128)S(1)} %get-tuple-element.14), channel_id=1, source_target_pairs={{0,32},{32,64},{64,96},{96,128},{128,160},{160,192},{192,224},{1,3... | collective-permute-start | bytes 196616 | tf_op jit(solution)/shard_map/ppermute | solution.py:182
  12.7 5.6 %collective-permute-start.2 = (f32[32,128]{1,0:T(8,128)S(1)}, f32[32,128]{1,0:T(8,128)S(1)}, u32[]{:S(2)}, u32[]{:S(2)}) collective-permute-start(f32[32,128]{1,0:T(8,128)S(1)} %get-tuple-element.12), channel_id=1, source_target_pairs={{0,256},{256,512},{512,768},{1,257},{257,513},{513,769},{2,258},{2... | collective-permute-start | bytes 49160 | tf_op jit(solution)/shard_map/ppermute | solution.py:182
  18.4 4.2 %collective-permute-start.3 = (f32[32,128]{1,0:T(8,128)S(1)}, f32[32,128]{1,0:T(8,128)S(1)}, u32[]{:S(2)}, u32[]{:S(2)}) collective-permute-start(f32[32,128]{1,0:T(8,128)S(1)} %get-tuple-element.13), channel_id=1, source_target_pairs={{256,0},{512,256},{768,512},{257,1},{513,257},{769,513},{258,2},{5... | collective-permute-start | bytes 49160 | tf_op jit(solution)/shard_map/ppermute | solution.py:182

commit v3 on v2

v3 whole, which is shorter than its diff:
```python
import functools

import jax
import jax.numpy as jnp
from jax import lax
from jax.experimental import pallas as pl
from jax.experimental.pallas import tpu as pltpu
from jax.sharding import PartitionSpec as P

E = 2.718281828459045
VMEM = pltpu.VMEM


def whole():
    return pl.BlockSpec(memory_space=VMEM)


def faces_kernel(steps, v_ref, own_ref, zlo_ref, zhi_ref, xlo_ref, xhi_ref, y_ref, sems):
    nz, nx, ny = v_ref.shape
    deep = nz // steps
    copies = []
    for i in range(steps):
        planes = slice(i * deep, (i + 1) * deep)
        copies.append(pltpu.make_async_copy(v_ref.at[planes], own_ref.at[planes], sems.at[i]))
        copies[-1].start()
    lane_pair = lax.broadcasted_iota(jnp.int32, (8, ny), 1) // 2
    for i in range(steps):
        copies[i].wait()
        for row in range(0, nx, 8):
            packed = jnp.zeros((8, ny), jnp.float32) if i == 0 else y_ref[row : row + 8, :]
            for z in range(i * deep, (i + 1) * deep):
                turned = pltpu.roll(own_ref[z, row : row + 8, :], 2 * z + 1, 1)
                packed = jnp.where(lane_pair == z, turned, packed)
            y_ref[row : row + 8, :] = packed
        for z in range(i * deep, (i + 1) * deep):
            xlo_ref[z : z + 1, :] = own_ref[z, 0:1, :]
            xhi_ref[z : z + 1, :] = own_ref[z, nx - 1 : nx, :]
    zlo_ref[...] = own_ref[0]
    zhi_ref[...] = own_ref[nz - 1]


def faces(volume):
    nz, nx, ny = volume.shape
    steps = 4
    plane = jax.ShapeDtypeStruct((nx, ny), jnp.float32)
    row = jax.ShapeDtypeStruct((nz, ny), jnp.float32)
    return pl.pallas_call(
        functools.partial(faces_kernel, steps),
        out_shape=(jax.ShapeDtypeStruct(volume.shape, jnp.float32), plane, plane, row, row, plane),
        in_specs=[pl.BlockSpec(memory_space=pltpu.HBM)],
        out_specs=[whole()] * 6,
        scratch_shapes=[pltpu.SemaphoreType.DMA((steps,))],
        compiler_params=pltpu.CompilerParams(vmem_limit_bytes=8 << 20),
        name="faces",
    )(pltpu.with_memory_space_constraint(volume, pltpu.HBM))


def weigh_kernel(scale, v_ref, red_ref, green_ref, blue_ref, clear_ref):
    nz, nx, ny = v_ref.shape
    height, unroll = 16, 16
    for start in range(0, nx, height):
        rows = slice(start, start + height)

        def group(k, clear):
            for i in range(unroll):
                z = k * unroll + i
                cur = v_ref[z, rows, :]
                grown = jnp.exp(cur)
                thick = grown * scale
                opacity = thick * (1.0 + thick * (-1.0 / 2 + thick * (1.0 / 6 + thick * (-1.0 / 24 + thick * (1.0 / 120)))))
                square = grown * grown
                up = square * E
                low = 1.0 + square * (1.0 / E)
                ratio = 1.0 / ((1.0 + up) * low)
                weight = clear * opacity
                share = weight * ratio
                red_ref[z, rows, :] = share * (up * low)
                green_ref[z, rows, :] = weight * jnp.exp(-cur * cur)
                blue_ref[z, rows, :] = share * (1.0 + up)
                clear = clear - weight
            return clear

        clear_ref[rows, :] = lax.fori_loop(0, nz // unroll, group, jnp.ones((height, ny), jnp.float32))


def weigh(volume, depth_cells):
    nz, nx, ny = volume.shape
    brick = jax.ShapeDtypeStruct(volume.shape, jnp.float32)
    return pl.pallas_call(
        functools.partial(weigh_kernel, 2.0 / depth_cells),
        out_shape=(brick, brick, brick, jax.ShapeDtypeStruct((nx, ny), jnp.float32)),
        in_specs=[whole()],
        out_specs=[whole()] * 4,
        compiler_params=pltpu.CompilerParams(vmem_limit_bytes=12 << 20),
        cost_estimate=pl.CostEstimate(flops=30 * nz * nx * ny, bytes_accessed=16 * nz * nx * ny, transcendentals=3 * nz * nx * ny),
        name="weigh",
    )(volume)


def shade_kernel(v_ref, red_ref, green_ref, blue_ref, clear_ref, zlo_ref, zhi_ref, xlo_ref, xhi_ref, ylo_ref, yhi_ref, out_ref):
    nz, nx, ny = v_ref.shape
    pieces = out_ref.shape[0]
    height, unroll = nx // pieces, 16
    col = lax.broadcasted_iota(jnp.int32, (height, ny), 1)
    line = lax.broadcasted_iota(jnp.int32, (height, ny), 0)
    odd = col % 2 == 1
    for block in range(pieces):
        start = block * height
        rows = slice(start, start + height)
        edge = jnp.where(odd, pltpu.roll(ylo_ref[rows, :], 1, 1), pltpu.roll(yhi_ref[rows, :], ny - 1, 1))

        def step(z, prev, cur, new, sums):
            if block == 0:
                above = jnp.where(line == 0, xlo_ref[pl.ds(z, 1), :], pltpu.roll(cur, 1, 0))
            else:
                above = v_ref[z, start - 1 : start - 1 + height, :]
            if block == pieces - 1:
                below = jnp.where(line == height - 1, xhi_ref[pl.ds(z, 1), :], pltpu.roll(cur, height - 1, 0))
            else:
                below = v_ref[z, start + 1 : start + 1 + height, :]
            outer = pltpu.roll(edge, ny - 1 - 2 * z, 1)
            left = jnp.where(col == 0, outer, pltpu.roll(cur, 1, 1))
            right = jnp.where(col == ny - 1, outer, pltpu.roll(cur, ny - 1, 1))
            dz = new - prev
            dx = below - above
            dy = right - left
            facing = jnp.abs(2.0 * (dz + dy) + dx)
            shading = 0.2 + (2.0 / 3.0) * facing * lax.rsqrt(dz * dz + dx * dx + dy * dy + 4.0)
            return tuple(s + ref[z, rows, :] * shading for s, ref in zip(sums, (red_ref, green_ref, blue_ref)))

        def group(k, carry):
            prev, cur, sums = carry
            for i in range(unroll):
                z = k * unroll + i
                new = v_ref[z + 1, rows, :]
                sums = step(z, prev, cur, new, sums)
                prev, cur = cur, new
            return prev, cur, sums

        zero = jnp.zeros((height, ny), jnp.float32)
        prev, cur, sums = lax.fori_loop(0, nz // unroll - 1, group, (zlo_ref[rows, :], v_ref[0, rows, :], (zero,) * 3))
        for z in range(nz - unroll, nz):
            new = v_ref[z + 1, rows, :] if z + 1 < nz else zhi_ref[rows, :]
            sums = step(z, prev, cur, new, sums)
            prev, cur = cur, new
        for c, value in enumerate((*sums, clear_ref[rows, :])):
            out_ref[block, c * height : (c + 1) * height, :] = value


def shade(volume, weights, halo, pieces):
    nz, nx, ny = volume.shape
    return pl.pallas_call(
        shade_kernel,
        out_shape=jax.ShapeDtypeStruct((pieces, 4 * nx // pieces, ny), jnp.float32),
        in_specs=[whole()] * 11,
        out_specs=whole(),
        compiler_params=pltpu.CompilerParams(vmem_limit_bytes=12 << 20),
        name="shade",
    )(volume, *weights, *halo)


def merge_kernel(final, parts_ref, out_ref):
    count, rows, ny = parts_ref.shape
    part = rows // 4
    clear = parts_ref[0, 3 * part :, :]
    total = [parts_ref[0, c * part : (c + 1) * part, :] for c in range(3)]
    for k in range(1, count):
        for c in range(3):
            total[c] = total[c] + clear * parts_ref[k, c * part : (c + 1) * part, :]
        clear = clear * parts_ref[k, 3 * part :, :]
    total.append(1.0 - clear if final else clear)
    for k in range(out_ref.shape[0]):
        for c in range(4):
            out_ref[k, c * part : (c + 1) * part, :] = total[c]


def merge(parts, copies, final):
    _, rows, ny = parts.shape
    return pl.pallas_call(
        functools.partial(merge_kernel, final),
        out_shape=jax.ShapeDtypeStruct((copies, rows, ny), jnp.float32),
        in_specs=[whole()],
        out_specs=whole(),
        compiler_params=pltpu.CompilerParams(vmem_limit_bytes=8 << 20),
        name="merge",
    )(parts)


def lay_kernel(parts_ref, out_ref):
    count, rows, ny = parts_ref.shape
    part = rows // 4
    for k in range(count):
        for c in range(4):
            out_ref[c, k * part : (k + 1) * part, :] = parts_ref[k, c * part : (c + 1) * part, :]


def lay(parts):
    count, rows, ny = parts.shape
    return pl.pallas_call(
        lay_kernel,
        out_shape=jax.ShapeDtypeStruct((4, count * rows // 4, ny), jnp.float32),
        in_specs=[whole()],
        out_specs=whole(),
        compiler_params=pltpu.CompilerParams(vmem_limit_bytes=8 << 20),
        name="lay",
    )(parts)


def shift(array, axis, upward):
    devices = lax.axis_size(axis)
    pairs = [(i, i + 1) if upward else (i + 1, i) for i in range(devices - 1)]
    return lax.ppermute(array, axis, pairs)


def per_device(volume):
    bricks = lax.axis_size("gz")
    depth_cells = volume.shape[0] * bricks
    own, zlo, zhi, xlo, xhi, y = faces(volume)
    front = shift(zhi, "gz", True)
    back = shift(zlo, "gz", False)
    first = shift(y, "gy", True)
    last = shift(y, "gy", False)
    above = shift(xhi, "gx", True)
    xlo, front = lax.optimization_barrier((xlo, front))
    below = shift(xlo, "gx", False)
    halo = (front, back, above, below, first, last)
    near = max(n for n in (1, 2, 4, 8) if bricks % n == 0)
    far = bricks // near
    runs = [[g * near + i for i in range(near)] for g in range(far)]
    strides = [[g * near + i for g in range(far)] for i in range(near)]
    parts = shade(own, weigh(own, depth_cells), halo, near)
    parts = lax.all_to_all(parts, "gz", 0, 0, axis_index_groups=runs)
    parts = merge(parts, far, False)
    parts = lax.all_to_all(parts, "gz", 0, 0, axis_index_groups=strides)
    parts = merge(parts, near, True)
    return lay(lax.all_to_all(parts, "gz", 0, 0, axis_index_groups=runs))


def solution(mesh):
    return jax.shard_map(
        per_device,
        mesh=mesh,
        in_specs=(P("gz", "gx", "gy"),),
        out_specs=P(None, "gx", "gy"),
        check_vma=False,
    )
```

time: 129 us -> 121 us (0.938); the launches traced: 127 us -> 121 us
  waiting for transfers between devices: 5.77 us -> 0.02 us
  Pallas kernels: 9.72 us -> 7.1 us
  starting transfers between devices: 13.5 us -> 15.3 us
  blocking collectives: 96.5 us -> 98.2 us
  local copies, waits for them, and re-layouts: 1.59 us -> 0 us
    ppermute x6, waiting for transfers between devices: 5.77 us -> 0.02 us  [shift(): return lax.ppermute(array, axis, pairs)]
    pallas_call x2 -> x3, Pallas kernels: 8.96 us -> 6.34 us  [the longest x1 2.27 us: shade(): pl.pallas_call(shade_kernel, out_shape=jax.ShapeDtypeStruct((pieces, 4 *...]
    all_to_all x1, blocking collectives: 21 us -> 23.5 us  [per_device(): return lay(lax.all_to_all(parts, 'gz', 0, 0, axis_index_groups=runs))]
    ppermute x6, starting transfers between devices: 13.5 us -> 15.3 us  [shift(): return lax.ppermute(array, axis, pairs)]
    unnamed x4 -> x0, local copies, waits for them, and re-layouts: 1.59 us -> none
  transfers between devices with their start and end apart: 6 -> 6, of which waited for: 2 -> 0; matrix products, arithmetic and copies ran while one was open for 0% -> 0% of each run, Pallas kernels for 0% -> 2%
where the time goes in v3:
time: 121 us
  blocking collectives  98.2 us (81%)
  starting transfers between devices  15.3 us (13%)
  Pallas kernels  7.1 us (6%)
    all_to_all x1, blocking collectives, per_device(): parts = lax.all_to_all(parts, 'gz', 0, 0, axis_index_groups=strides)  44.1 us
    all_to_all x1, blocking collectives, per_device(): parts = lax.all_to_all(parts, 'gz', 0, 0, axis_index_groups=runs)  30.6 us
    all_to_all x1, blocking collectives, per_device(): return lay(lax.all_to_all(parts, 'gz', 0, 0, axis_index_groups=runs))  23.5 us
    ppermute x6, starting transfers between devices, shift(): return lax.ppermute(array, axis, pairs)  15.3 us
  transfers between devices with their start and end apart: 6, of which 0 were waited for; matrix products, arithmetic and copies ran while one was open for 0% of the time, Pallas kernels for 2%

profile of v3, /device:TPU:6, one launch (start us, length us, event | category | flops | bytes accessed | tf_op | source)
XLA Modules:
  0.0 120.7 jit_solution(7993205326791609427)
XLA Ops:
  0.0 1.9 %faces.1 = (f32[32,128,128]{2,1,0:T(8,128)S(1)}, f32[128,128]{1,0:T(8,128)S(1)}, f32[128,128]{1,0:T(8,128)S(1)}, f32[32,128]{1,0:T(8,128)S(1)}, f32[32,128]{1,0:T(8,128)S(1)}, /*index=5*/f32[128,128]{1,0:T(8,128)S(1)}) custom-call(f32[32,128,128]{2,1,0:T(8,128)} %v_ref.1), custom_call_target="tpu_custom_call" | custom-call | tf_op jit(solution)/shard_map/faces/pallas_call | solution.py:47
  1.9 3.8 %collective-permute-start = (f32[128,128]{1,0:T(8,128)S(1)}, f32[128,128]{1,0:T(8,128)S(1)}, u32[]{:S(2)}, u32[]{:S(2)}) collective-permute-start(f32[128,128]{1,0:T(8,128)S(1)} %get-tuple-element.23), channel_id=1, source_target_pairs={{0,1},{1,2},{2,3},{3,4},{4,5},{5,6},{6,7},{7,8},{8,9},{9,10},{10,1... | collective-permute-start | bytes 196616 | tf_op jit(solution)/shard_map/ppermute | solution.py:212
  5.8 1.3 %collective-permute-start.1 = (f32[128,128]{1,0:T(8,128)S(1)}, f32[128,128]{1,0:T(8,128)S(1)}, u32[]{:S(2)}, u32[]{:S(2)}) collective-permute-start(f32[128,128]{1,0:T(8,128)S(1)} %get-tuple-element.25), channel_id=1, source_target_pairs={{1,0},{2,1},{3,2},{4,3},{5,4},{6,5},{7,6},{8,7},{9,8},{10,9},{11,1... | collective-permute-start | bytes 196616 | tf_op jit(solution)/shard_map/ppermute | solution.py:212
  7.1 1.3 %collective-permute-start.5 = (f32[128,128]{1,0:T(8,128)S(1)}, f32[128,128]{1,0:T(8,128)S(1)}, u32[]{:S(2)}, u32[]{:S(2)}) collective-permute-start(f32[128,128]{1,0:T(8,128)S(1)} %get-tuple-element.28), channel_id=1, source_target_pairs={{32,0},{64,32},{96,64},{128,96},{160,128},{192,160},{224,192},{33,... | collective-permute-start | bytes 196616 | tf_op jit(solution)/shard_map/ppermute | solution.py:212
  8.4 3.0 %collective-permute-start.4 = (f32[128,128]{1,0:T(8,128)S(1)}, f32[128,128]{1,0:T(8,128)S(1)}, u32[]{:S(2)}, u32[]{:S(2)}) collective-permute-start(f32[128,128]{1,0:T(8,128)S(1)} %get-tuple-element.28), channel_id=1, source_target_pairs={{0,32},{32,64},{64,96},{96,128},{128,160},{160,192},{192,224},{1,3... | collective-permute-start | bytes 196616 | tf_op jit(solution)/shard_map/ppermute | solution.py:212
  11.4 1.3 %collective-permute-start.2 = (f32[32,128]{1,0:T(8,128)S(1)}, f32[32,128]{1,0:T(8,128)S(1)}, u32[]{:S(2)}, u32[]{:S(2)}) collective-permute-start(f32[32,128]{1,0:T(8,128)S(1)} %get-tuple-element.26), channel_id=1, source_target_pairs={{0,256},{256,512},{512,768},{1,257},{257,513},{513,769},{2,258},{2... | collective-permute-start | bytes 49160 | tf_op jit(solution)/shard_map/ppermute | solution.py:212
  12.7 0.0 collective-permute-done.zlo_ref
  12.7 4.5 %collective-permute-start.3 = (f32[32,128]{1,0:T(8,128)S(1)}, f32[32,128]{1,0:T(8,128)S(1)}, u32[]{:S(2)}, u32[]{:S(2)}) collective-permute-start(f32[32,128]{1,0:T(8,128)S(1)} %get-tuple-element.27), channel_id=1, source_target_pairs={{256,0},{512,256},{768,512},{257,1},{513,257},{769,513},{258,2},{5... | collective-permute-start | bytes 49160 | tf_op jit(solution)/shard_map/ppermute | solution.py:212
  17.3 2.1 %weigh.1 = (f32[32,128,128]{2,1,0:T(8,128)S(1)}, f32[32,128,128]{2,1,0:T(8,128)S(1)}, f32[32,128,128]{2,1,0:T(8,128)S(1)}, f32[128,128]{1,0:T(8,128)S(1)}) custom-call(f32[32,128,128]{2,1,0:T(8,128)S(1)} %get-tuple-element.17.v_ref), custom_call_target="tpu_custom_call" | custom-call | flops 15728640 | bytes 8388608 | tf_op jit(solution)/shard_map/weigh/pallas_call | solution.py:89
  19.4 0.0 collective-permute-done.2.xlo_ref
  19.4 0.0 collective-permute-done.1.zhi_ref
  19.4 0.0 collective-permute-done.5.yhi_ref
  19.5 0.0 collective-permute-done.4.ylo_ref
  19.5 0.0 collective-permute-done.3.xhi_ref
  19.5 2.3 %shade.1 = f32[8,64,128]{2,1,0:T(8,128)S(1)} custom-call(f32[32,128,128]{2,1,0:T(8,128)S(1)} %get-tuple-element.17.v_ref, f32[32,128,128]{2,1,0:T(8,128)S(1)} %get-tuple-element.18.red_ref, f32[32,128,128]{2,1,0:T(8,128)S(1)} %get-tuple-element.19.green_ref, f32[32,128,128]{2,1,0:T(8,128)S(1)} %get-tuple-element.20.blue_ref, ...), custom_call_target="tpu_custom_call" | custom-call | tf_op jit(solution)/shard_map/shade/pallas_call | solution.py:152
  21.8 30.6 %all_to_all.15.parts_ref = f32[8,64,128]{2,1,0:T(8,128)S(1)} all-to-all(f32[8,64,128]{2,1,0:T(8,128)S(1)} %shade.1), channel_id=1, replica_groups={{0,1,2,3,4,5,6,7},{8,9,10,11,12,13,14,15},{16,17,18,19,20,21,22,23},{24..., dimensions={0} | all-to-all | bytes 524288 | tf_op jit(solution)/shard_map/all_to_all | solution.py:232
  52.4 44.1 %all_to_all.16.parts_ref = f32[4,64,128]{2,1,0:T(8,128)S(1)} all-to-all(f32[4,64,128]{2,1,0:T(8,128)S(1)} %merge.2), channel_id=1, replica_groups={{0,8,16,24},{1,9,17,25},{2,10,18,26},{3,11,19,27},{4,12,20,28},{5,13,21..., dimensions={0} | all-to-all | bytes 262144 | tf_op jit(solution)/shard_map/all_to_all | solution.py:234
  96.5 23.5 %all_to_all.17.parts_ref = f32[8,64,128]{2,1,0:T(8,128)S(1)} all-to-all(f32[8,64,128]{2,1,0:T(8,128)S(1)} %merge.3), channel_id=1, replica_groups={{0,1,2,3,4,5,6,7},{8,9,10,11,12,13,14,15},{16,17,18,19,20,21,22,23},{24..., dimensions={0} | all-to-all | bytes 524288 | tf_op jit(solution)/shard_map/all_to_all | solution.py:236
  120.0 0.7 lay.1
  (2 shorter events, 0.0 us)
Async XLA Ops:
  1.9 10.8 %collective-permute-start = (f32[128,128]{1,0:T(8,128)S(1)}, f32[128,128]{1,0:T(8,128)S(1)}, u32[]{:S(2)}, u32[]{:S(2)}) collective-permute-start(f32[128,128]{1,0:T(8,128)S(1)} %get-tuple-element.23), channel_id=1, source_target_pairs={{0,1},{1,2},{2,3},{3,4},{4,5},{5,6},{6,7},{7,8},{8,9},{9,10},{10,1... | collective-permute-start | bytes 196616 | tf_op jit(solution)/shard_map/ppermute | solution.py:212
  5.8 13.7 %collective-permute-start.1 = (f32[128,128]{1,0:T(8,128)S(1)}, f32[128,128]{1,0:T(8,128)S(1)}, u32[]{:S(2)}, u32[]{:S(2)}) collective-permute-start(f32[128,128]{1,0:T(8,128)S(1)} %get-tuple-element.25), channel_id=1, source_target_pairs={{1,0},{2,1},{3,2},{4,3},{5,4},{6,5},{7,6},{8,7},{9,8},{10,9},{11,1... | collective-permute-start | bytes 196616 | tf_op jit(solution)/shard_map/ppermute | solution.py:212
  7.1 12.4 %collective-permute-start.5 = (f32[128,128]{1,0:T(8,128)S(1)}, f32[128,128]{1,0:T(8,128)S(1)}, u32[]{:S(2)}, u32[]{:S(2)}) collective-permute-start(f32[128,128]{1,0:T(8,128)S(1)} %get-tuple-element.28), channel_id=1, source_target_pairs={{32,0},{64,32},{96,64},{128,96},{160,128},{192,160},{224,192},{33,... | collective-permute-start | bytes 196616 | tf_op jit(solution)/shard_map/ppermute | solution.py:212
  8.4 11.1 %collective-permute-start.4 = (f32[128,128]{1,0:T(8,128)S(1)}, f32[128,128]{1,0:T(8,128)S(1)}, u32[]{:S(2)}, u32[]{:S(2)}) collective-permute-start(f32[128,128]{1,0:T(8,128)S(1)} %get-tuple-element.28), channel_id=1, source_target_pairs={{0,32},{32,64},{64,96},{96,128},{128,160},{160,192},{192,224},{1,3... | collective-permute-start | bytes 196616 | tf_op jit(solution)/shard_map/ppermute | solution.py:212
  11.4 8.0 %collective-permute-start.2 = (f32[32,128]{1,0:T(8,128)S(1)}, f32[32,128]{1,0:T(8,128)S(1)}, u32[]{:S(2)}, u32[]{:S(2)}) collective-permute-start(f32[32,128]{1,0:T(8,128)S(1)} %get-tuple-element.26), channel_id=1, source_target_pairs={{0,256},{256,512},{512,768},{1,257},{257,513},{513,769},{2,258},{2... | collective-permute-start | bytes 49160 | tf_op jit(solution)/shard_map/ppermute | solution.py:212
  12.7 6.8 %collective-permute-start.3 = (f32[32,128]{1,0:T(8,128)S(1)}, f32[32,128]{1,0:T(8,128)S(1)}, u32[]{:S(2)}, u32[]{:S(2)}) collective-permute-start(f32[32,128]{1,0:T(8,128)S(1)} %get-tuple-element.27), channel_id=1, source_target_pairs={{256,0},{512,256},{768,512},{257,1},{513,257},{769,513},{258,2},{5... | collective-permute-start | bytes 49160 | tf_op jit(solution)/shard_map/ppermute | solution.py:212

commit v4 on v3

--- a/solution.py
+++ b/solution.py
@@ -97,66 +97,87 @@
     )(volume)
 
 
-def shade_kernel(v_ref, red_ref, green_ref, blue_ref, clear_ref, zlo_ref, zhi_ref, xlo_ref, xhi_ref, ylo_ref, yhi_ref, out_ref):
+def shade_rows(v_ref, weight_refs, clear_ref, zlo_ref, zhi_ref, ylo_ref, yhi_ref, out_ref, block, xlo_ref=None, xhi_ref=None):
     nz, nx, ny = v_ref.shape
-    pieces = out_ref.shape[0]
-    height, unroll = nx // pieces, 16
+    height, unroll = nx // out_ref.shape[0], 16
     col = lax.broadcasted_iota(jnp.int32, (height, ny), 1)
     line = lax.broadcasted_iota(jnp.int32, (height, ny), 0)
-    odd = col % 2 == 1
-    for block in range(pieces):
-        start = block * height
-        rows = slice(start, start + height)
-        edge = jnp.where(odd, pltpu.roll(ylo_ref[rows, :], 1, 1), pltpu.roll(yhi_ref[rows, :], ny - 1, 1))
-
-        def step(z, prev, cur, new, sums):
-            if block == 0:
-                above = jnp.where(line == 0, xlo_ref[pl.ds(z, 1), :], pltpu.roll(cur, 1, 0))
-            else:
-                above = v_ref[z, start - 1 : start - 1 + height, :]
-            if block == pieces - 1:
-                below = jnp.where(line == height - 1, xhi_ref[pl.ds(z, 1), :], pltpu.roll(cur, height - 1, 0))
-            else:
-                below = v_ref[z, start + 1 : start + 1 + height, :]
-            outer = pltpu.roll(edge, ny - 1 - 2 * z, 1)
-            left = jnp.where(col == 0, outer, pltpu.roll(cur, 1, 1))
-            right = jnp.where(col == ny - 1, outer, pltpu.roll(cur, ny - 1, 1))
-            dz = new - prev
-            dx = below - above
-            dy = right - left
-            facing = jnp.abs(2.0 * (dz + dy) + dx)
-            shading = 0.2 + (2.0 / 3.0) * facing * lax.rsqrt(dz * dz + dx * dx + dy * dy + 4.0)
-            return tuple(s + ref[z, rows, :] * shading for s, ref in zip(sums, (red_ref, green_ref, blue_ref)))
-
-        def group(k, carry):
-            prev, cur, sums = carry
-            for i in range(unroll):
-                z = k * unroll + i
-                new = v_ref[z + 1, rows, :]
-                sums = step(z, prev, cur, new, sums)
-                prev, cur = cur, new
-            return prev, cur, sums
-
-        zero = jnp.zeros((height, ny), jnp.float32)
-        prev, cur, sums = lax.fori_loop(0, nz // unroll - 1, group, (zlo_ref[rows, :], v_ref[0, rows, :], (zero,) * 3))
-        for z in range(nz - unroll, nz):
-            new = v_ref[z + 1, rows, :] if z + 1 < nz else zhi_ref[rows, :]
+    start = block * height
+    rows = slice(start, start + height)
+    edge = jnp.where(col % 2 == 1, pltpu.roll(ylo_ref[rows, :], 1, 1), pltpu.roll(yhi_ref[rows, :], ny - 1, 1))
+
+    def step(z, prev, cur, new, sums):
+        if start == 0:
+            above = jnp.where(line == 0, xlo_ref[pl.ds(z, 1), :], pltpu.roll(cur, 1, 0))
+        else:
+            above = v_ref[z, start - 1 : start - 1 + height, :]
+        if start + height == nx:
+            below = jnp.where(line == height - 1, xhi_ref[pl.ds(z, 1), :], pltpu.roll(cur, height - 1, 0))
+        else:
+            below = v_ref[z, start + 1 : start + 1 + height, :]
+        outer = pltpu.roll(edge, ny - 1 - 2 * z, 1)
+        left = jnp.where(col == 0, outer, pltpu.roll(cur, 1, 1))
+        right = jnp.where(col == ny - 1, outer, pltpu.roll(cur, ny - 1, 1))
+        dz = new - prev
+        dx = below - above
+        dy = right - left
+        facing = jnp.abs(2.0 * (dz + dy) + dx)
+        shading = 0.2 + (2.0 / 3.0) * facing * lax.rsqrt(dz * dz + dx * dx + dy * dy + 4.0)
+        return tuple(s + ref[z, rows, :] * shading for s, ref in zip(sums, weight_refs))
+
+    def group(k, carry):
+        prev, cur, sums = carry
+        for i in range(unroll):
+            z = k * unroll + i
+            new = v_ref[z + 1, rows, :]
             sums = step(z, prev, cur, new, sums)
             prev, cur = cur, new
-        for c, value in enumerate((*sums, clear_ref[rows, :])):
-            out_ref[block, c * height : (c + 1) * height, :] = value
+        return prev, cur, sums
+
+    zero = jnp.zeros((height, ny), jnp.float32)
+    prev, cur, sums = lax.fori_loop(0, nz // unroll - 1, group, (zlo_ref[rows, :], v_ref[0, rows, :], (zero,) * 3))
+    for z in range(nz - unroll, nz):
+        new = v_ref[z + 1, rows, :] if z + 1 < nz else zhi_ref[rows, :]
+        sums = step(z, prev, cur, new, sums)
+        prev, cur = cur, new
+    for c, value in enumerate((*sums, clear_ref[rows, :])):
+        out_ref[block, c * height : (c + 1) * height, :] = value
+
+
+def inner_kernel(v_ref, red_ref, green_ref, blue_ref, clear_ref, zlo_ref, zhi_ref, ylo_ref, yhi_ref, out_ref):
+    for block in range(1, out_ref.shape[0] - 1):
+        shade_rows(v_ref, (red_ref, green_ref, blue_ref), clear_ref, zlo_ref, zhi_ref, ylo_ref, yhi_ref, out_ref, block)
+
+
+def outer_kernel(v_ref, red_ref, green_ref, blue_ref, clear_ref, zlo_ref, zhi_ref, ylo_ref, yhi_ref, xlo_ref, xhi_ref, inner_ref, out_ref):
+    pieces = out_ref.shape[0]
+    out_ref[1 : pieces - 1] = inner_ref[1 : pieces - 1]
+    for block in (0, pieces - 1):
+        shade_rows(v_ref, (red_ref, green_ref, blue_ref), clear_ref, zlo_ref, zhi_ref, ylo_ref, yhi_ref, out_ref, block, xlo_ref, xhi_ref)
 
 
 def shade(volume, weights, halo, pieces):
     nz, nx, ny = volume.shape
-    return pl.pallas_call(
-        shade_kernel,
-        out_shape=jax.ShapeDtypeStruct((pieces, 4 * nx // pieces, ny), jnp.float32),
-        in_specs=[whole()] * 11,
+    out = jax.ShapeDtypeStruct((pieces, 4 * nx // pieces, ny), jnp.float32)
+    front, back, above, below, first, last = halo
+    cells = nz * nx * ny
+    inner = pl.pallas_call(
+        inner_kernel,
+        out_shape=out,
+        in_specs=[whole()] * 9,
         out_specs=whole(),
         compiler_params=pltpu.CompilerParams(vmem_limit_bytes=12 << 20),
-        name="shade",
-    )(volume, *weights, *halo)
+        cost_estimate=pl.CostEstimate(flops=30 * cells, bytes_accessed=16 * cells, transcendentals=cells),
+        name="shade_inner",
+    )(volume, *weights, front, back, first, last)
+    return pl.pallas_call(
+        outer_kernel,
+        out_shape=out,
+        in_specs=[whole()] * 12,
+        out_specs=whole(),
+        compiler_params=pltpu.CompilerParams(vmem_limit_bytes=12 << 20),
+        name="shade_outer",
+    )(volume, *weights, front, back, first, last, above, below, inner)
 
 
 def merge_kernel(final, parts_ref, out_ref):

time: 121 us -> 121 us (level)
  transfers between devices with their start and end apart: 6 -> 6, of which waited for: 0 -> 0; matrix products, arithmetic and copies ran while one was open for 0% -> 0% of each run, Pallas kernels for 2% -> 3%
where the time goes in v4:
time: 121 us
  blocking collectives  98.2 us (81%)
  starting transfers between devices  15.3 us (13%)
  Pallas kernels  7.17 us (6%)
    all_to_all x1, blocking collectives, per_device(): parts = lax.all_to_all(parts, 'gz', 0, 0, axis_index_groups=strides)  44.1 us
    all_to_all x1, blocking collectives, per_device(): parts = lax.all_to_all(parts, 'gz', 0, 0, axis_index_groups=runs)  30.6 us
    all_to_all x1, blocking collectives, per_device(): return lay(lax.all_to_all(parts, 'gz', 0, 0, axis_index_groups=runs))  23.5 us
    ppermute x6, starting transfers between devices, shift(): return lax.ppermute(array, axis, pairs)  15.3 us
  transfers between devices with their start and end apart: 6, of which 0 were waited for; matrix products, arithmetic and copies ran while one was open for 0% of the time, Pallas kernels for 3%

profile of v4, /device:TPU:6, one launch (start us, length us, event | category | flops | bytes accessed | tf_op | source)
XLA Modules:
  0.0 120.8 jit_solution(9371756788750813382)
XLA Ops:
  0.0 1.9 %faces.1 = (f32[32,128,128]{2,1,0:T(8,128)S(1)}, f32[128,128]{1,0:T(8,128)S(1)}, f32[128,128]{1,0:T(8,128)S(1)}, f32[32,128]{1,0:T(8,128)S(1)}, f32[32,128]{1,0:T(8,128)S(1)}, /*index=5*/f32[128,128]{1,0:T(8,128)S(1)}) custom-call(f32[32,128,128]{2,1,0:T(8,128)} %v_ref.1), custom_call_target="tpu_custom_call" | custom-call | tf_op jit(solution)/shard_map/faces/pallas_call | solution.py:47
  1.9 3.8 %collective-permute-start = (f32[128,128]{1,0:T(8,128)S(1)}, f32[128,128]{1,0:T(8,128)S(1)}, u32[]{:S(2)}, u32[]{:S(2)}) collective-permute-start(f32[128,128]{1,0:T(8,128)S(1)} %get-tuple-element.23), channel_id=1, source_target_pairs={{0,1},{1,2},{2,3},{3,4},{4,5},{5,6},{6,7},{7,8},{8,9},{9,10},{10,1... | collective-permute-start | bytes 196616 | tf_op jit(solution)/shard_map/ppermute | solution.py:233
  5.8 1.3 %collective-permute-start.1 = (f32[128,128]{1,0:T(8,128)S(1)}, f32[128,128]{1,0:T(8,128)S(1)}, u32[]{:S(2)}, u32[]{:S(2)}) collective-permute-start(f32[128,128]{1,0:T(8,128)S(1)} %get-tuple-element.25), channel_id=1, source_target_pairs={{1,0},{2,1},{3,2},{4,3},{5,4},{6,5},{7,6},{8,7},{9,8},{10,9},{11,1... | collective-permute-start | bytes 196616 | tf_op jit(solution)/shard_map/ppermute | solution.py:233
  7.1 1.3 %collective-permute-start.3 = (f32[128,128]{1,0:T(8,128)S(1)}, f32[128,128]{1,0:T(8,128)S(1)}, u32[]{:S(2)}, u32[]{:S(2)}) collective-permute-start(f32[128,128]{1,0:T(8,128)S(1)} %get-tuple-element.26), channel_id=1, source_target_pairs={{32,0},{64,32},{96,64},{128,96},{160,128},{192,160},{224,192},{33,... | collective-permute-start | bytes 196616 | tf_op jit(solution)/shard_map/ppermute | solution.py:233
  8.4 3.0 %collective-permute-start.2 = (f32[128,128]{1,0:T(8,128)S(1)}, f32[128,128]{1,0:T(8,128)S(1)}, u32[]{:S(2)}, u32[]{:S(2)}) collective-permute-start(f32[128,128]{1,0:T(8,128)S(1)} %get-tuple-element.26), channel_id=1, source_target_pairs={{0,32},{32,64},{64,96},{96,128},{128,160},{160,192},{192,224},{1,3... | collective-permute-start | bytes 196616 | tf_op jit(solution)/shard_map/ppermute | solution.py:233
  11.4 1.3 %collective-permute-start.4 = (f32[32,128]{1,0:T(8,128)S(1)}, f32[32,128]{1,0:T(8,128)S(1)}, u32[]{:S(2)}, u32[]{:S(2)}) collective-permute-start(f32[32,128]{1,0:T(8,128)S(1)} %get-tuple-element.27), channel_id=1, source_target_pairs={{0,256},{256,512},{512,768},{1,257},{257,513},{513,769},{2,258},{2... | collective-permute-start | bytes 49160 | tf_op jit(solution)/shard_map/ppermute | solution.py:233
  12.7 0.0 collective-permute-done.zlo_ref
  12.7 4.5 %collective-permute-start.5 = (f32[32,128]{1,0:T(8,128)S(1)}, f32[32,128]{1,0:T(8,128)S(1)}, u32[]{:S(2)}, u32[]{:S(2)}) collective-permute-start(f32[32,128]{1,0:T(8,128)S(1)} %get-tuple-element.28), channel_id=1, source_target_pairs={{256,0},{512,256},{768,512},{257,1},{513,257},{769,513},{258,2},{5... | collective-permute-start | bytes 49160 | tf_op jit(solution)/shard_map/ppermute | solution.py:233
  17.3 2.1 %weigh.1 = (f32[32,128,128]{2,1,0:T(8,128)S(1)}, f32[32,128,128]{2,1,0:T(8,128)S(1)}, f32[32,128,128]{2,1,0:T(8,128)S(1)}, f32[128,128]{1,0:T(8,128)S(1)}) custom-call(f32[32,128,128]{2,1,0:T(8,128)S(1)} %get-tuple-element.17.v_ref), custom_call_target="tpu_custom_call" | custom-call | flops 15728640 | bytes 8388608 | tf_op jit(solution)/shard_map/weigh/pallas_call | solution.py:89
  19.4 0.0 collective-permute-done.1.zhi_ref
  19.4 0.0 collective-permute-done.3.yhi_ref
  19.4 0.0 collective-permute-done.2.ylo_ref
  19.5 1.7 %shade_inner.1.inner_ref = f32[8,64,128]{2,1,0:T(8,128)S(1)} custom-call(f32[32,128,128]{2,1,0:T(8,128)S(1)} %get-tuple-element.17.v_ref, f32[32,128,128]{2,1,0:T(8,128)S(1)} %get-tuple-element.18.red_ref, f32[32,128,128]{2,1,0:T(8,128)S(1)} %get-tuple-element.19.green_ref, f32[32,128,128]{2,1,0:T(8,128)S(1)} %get-tuple-element.20.blue_ref, ...), custom_call_target="tpu_custom_call" | custom-call | flops 15728640 | bytes 8388608 | tf_op jit(solution)/shard_map/shade_inner/pallas_call | solution.py:164
  21.2 0.0 collective-permute-done.4.xlo_ref
  21.2 0.0 collective-permute-done.5.xhi_ref
  21.2 0.6 shade_outer.1
  21.8 30.6 %all_to_all.15.parts_ref = f32[8,64,128]{2,1,0:T(8,128)S(1)} all-to-all(f32[8,64,128]{2,1,0:T(8,128)S(1)} %shade_outer.1), channel_id=1, replica_groups={{0,1,2,3,4,5,6,7},{8,9,10,11,12,13,14,15},{16,17,18,19,20,21,22,23},{24..., dimensions={0} | all-to-all | bytes 524288 | tf_op jit(solution)/shard_map/all_to_all | solution.py:253
  52.5 44.1 %all_to_all.16.parts_ref = f32[4,64,128]{2,1,0:T(8,128)S(1)} all-to-all(f32[4,64,128]{2,1,0:T(8,128)S(1)} %merge.2), channel_id=1, replica_groups={{0,8,16,24},{1,9,17,25},{2,10,18,26},{3,11,19,27},{4,12,20,28},{5,13,21..., dimensions={0} | all-to-all | bytes 262144 | tf_op jit(solution)/shard_map/all_to_all | solution.py:255
  96.6 23.5 %all_to_all.17.parts_ref = f32[8,64,128]{2,1,0:T(8,128)S(1)} all-to-all(f32[8,64,128]{2,1,0:T(8,128)S(1)} %merge.3), channel_id=1, replica_groups={{0,1,2,3,4,5,6,7},{8,9,10,11,12,13,14,15},{16,17,18,19,20,21,22,23},{24..., dimensions={0} | all-to-all | bytes 524288 | tf_op jit(solution)/shard_map/all_to_all | solution.py:257
  120.1 0.7 lay.1
  (2 shorter events, 0.0 us)
Async XLA Ops:
  1.9 10.8 %collective-permute-start = (f32[128,128]{1,0:T(8,128)S(1)}, f32[128,128]{1,0:T(8,128)S(1)}, u32[]{:S(2)}, u32[]{:S(2)}) collective-permute-start(f32[128,128]{1,0:T(8,128)S(1)} %get-tuple-element.23), channel_id=1, source_target_pairs={{0,1},{1,2},{2,3},{3,4},{4,5},{5,6},{6,7},{7,8},{8,9},{9,10},{10,1... | collective-permute-start | bytes 196616 | tf_op jit(solution)/shard_map/ppermute | solution.py:233
  5.8 13.7 %collective-permute-start.1 = (f32[128,128]{1,0:T(8,128)S(1)}, f32[128,128]{1,0:T(8,128)S(1)}, u32[]{:S(2)}, u32[]{:S(2)}) collective-permute-start(f32[128,128]{1,0:T(8,128)S(1)} %get-tuple-element.25), channel_id=1, source_target_pairs={{1,0},{2,1},{3,2},{4,3},{5,4},{6,5},{7,6},{8,7},{9,8},{10,9},{11,1... | collective-permute-start | bytes 196616 | tf_op jit(solution)/shard_map/ppermute | solution.py:233
  7.1 12.4 %collective-permute-start.3 = (f32[128,128]{1,0:T(8,128)S(1)}, f32[128,128]{1,0:T(8,128)S(1)}, u32[]{:S(2)}, u32[]{:S(2)}) collective-permute-start(f32[128,128]{1,0:T(8,128)S(1)} %get-tuple-element.26), channel_id=1, source_target_pairs={{32,0},{64,32},{96,64},{128,96},{160,128},{192,160},{224,192},{33,... | collective-permute-start | bytes 196616 | tf_op jit(solution)/shard_map/ppermute | solution.py:233
  8.4 11.1 %collective-permute-start.2 = (f32[128,128]{1,0:T(8,128)S(1)}, f32[128,128]{1,0:T(8,128)S(1)}, u32[]{:S(2)}, u32[]{:S(2)}) collective-permute-start(f32[128,128]{1,0:T(8,128)S(1)} %get-tuple-element.26), channel_id=1, source_target_pairs={{0,32},{32,64},{64,96},{96,128},{128,160},{160,192},{192,224},{1,3... | collective-permute-start | bytes 196616 | tf_op jit(solution)/shard_map/ppermute | solution.py:233
  11.4 9.8 %collective-permute-start.4 = (f32[32,128]{1,0:T(8,128)S(1)}, f32[32,128]{1,0:T(8,128)S(1)}, u32[]{:S(2)}, u32[]{:S(2)}) collective-permute-start(f32[32,128]{1,0:T(8,128)S(1)} %get-tuple-element.27), channel_id=1, source_target_pairs={{0,256},{256,512},{512,768},{1,257},{257,513},{513,769},{2,258},{2... | collective-permute-start | bytes 49160 | tf_op jit(solution)/shard_map/ppermute | solution.py:233
  12.7 8.5 %collective-permute-start.5 = (f32[32,128]{1,0:T(8,128)S(1)}, f32[32,128]{1,0:T(8,128)S(1)}, u32[]{:S(2)}, u32[]{:S(2)}) collective-permute-start(f32[32,128]{1,0:T(8,128)S(1)} %get-tuple-element.28), channel_id=1, source_target_pairs={{256,0},{512,256},{768,512},{257,1},{513,257},{769,513},{258,2},{5... | collective-permute-start | bytes 49160 | tf_op jit(solution)/shard_map/ppermute | solution.py:233

commit v5 on v3

--- a/solution.py
+++ b/solution.py
@@ -15,7 +15,7 @@
     return pl.BlockSpec(memory_space=VMEM)
 
 
-def faces_kernel(steps, v_ref, own_ref, zlo_ref, zhi_ref, xlo_ref, xhi_ref, y_ref, sems):
+def faces_kernel(steps, v_ref, own_ref, pair_ref, rest_ref, xlo_ref, xhi_ref, y_ref, sems):
     nz, nx, ny = v_ref.shape
     deep = nz // steps
     copies = []
@@ -35,8 +35,9 @@
         for z in range(i * deep, (i + 1) * deep):
             xlo_ref[z : z + 1, :] = own_ref[z, 0:1, :]
             xhi_ref[z : z + 1, :] = own_ref[z, nx - 1 : nx, :]
-    zlo_ref[...] = own_ref[0]
-    zhi_ref[...] = own_ref[nz - 1]
+    odd = lax.rem(lax.axis_index("gz"), 2)
+    pair_ref[...] = own_ref[(1 - odd) * (nz - 1)]
+    rest_ref[...] = own_ref[odd * (nz - 1)]
 
 
 def faces(volume):
@@ -97,7 +98,9 @@
     )(volume)
 
 
-def shade_kernel(v_ref, red_ref, green_ref, blue_ref, clear_ref, zlo_ref, zhi_ref, xlo_ref, xhi_ref, ylo_ref, yhi_ref, out_ref):
+def shade_kernel(v_ref, red_ref, green_ref, blue_ref, clear_ref, zpair_ref, zrest_ref, xlo_ref, xhi_ref, ypair_ref, yrest_ref, out_ref):
+    odd_z = lax.rem(lax.axis_index("gz"), 2) == 1
+    odd_y = lax.rem(lax.axis_index("gy"), 2) == 1
     nz, nx, ny = v_ref.shape
     pieces = out_ref.shape[0]
     height, unroll = nx // pieces, 16
@@ -107,7 +110,11 @@
     for block in range(pieces):
         start = block * height
         rows = slice(start, start + height)
-        edge = jnp.where(odd, pltpu.roll(ylo_ref[rows, :], 1, 1), pltpu.roll(yhi_ref[rows, :], ny - 1, 1))
+        pair, rest = ypair_ref[rows, :], yrest_ref[rows, :]
+        before, after = jnp.where(odd_y, pair, rest), jnp.where(odd_y, rest, pair)
+        edge = jnp.where(odd, pltpu.roll(before, 1, 1), pltpu.roll(after, ny - 1, 1))
+        front = jnp.where(odd_z, zpair_ref[rows, :], zrest_ref[rows, :])
+        back = jnp.where(odd_z, zrest_ref[rows, :], zpair_ref[rows, :])
 
         def step(z, prev, cur, new, sums):
             if block == 0:
@@ -138,9 +145,9 @@
             return prev, cur, sums
 
         zero = jnp.zeros((height, ny), jnp.float32)
-        prev, cur, sums = lax.fori_loop(0, nz // unroll - 1, group, (zlo_ref[rows, :], v_ref[0, rows, :], (zero,) * 3))
+        prev, cur, sums = lax.fori_loop(0, nz // unroll - 1, group, (front, v_ref[0, rows, :], (zero,) * 3))
         for z in range(nz - unroll, nz):
-            new = v_ref[z + 1, rows, :] if z + 1 < nz else zhi_ref[rows, :]
+            new = v_ref[z + 1, rows, :] if z + 1 < nz else back
             sums = step(z, prev, cur, new, sums)
             prev, cur = cur, new
         for c, value in enumerate((*sums, clear_ref[rows, :])):
@@ -212,18 +219,23 @@
     return lax.ppermute(array, axis, pairs)
 
 
+def swap(array, axis, first):
+    lower = range(first, lax.axis_size(axis) - 1, 2)
+    return lax.ppermute(array, axis, [p for i in lower for p in ((i, i + 1), (i + 1, i))])
+
+
 def per_device(volume):
     bricks = lax.axis_size("gz")
     depth_cells = volume.shape[0] * bricks
-    own, zlo, zhi, xlo, xhi, y = faces(volume)
-    front = shift(zhi, "gz", True)
-    back = shift(zlo, "gz", False)
-    first = shift(y, "gy", True)
-    last = shift(y, "gy", False)
+    own, zpair, zrest, xlo, xhi, y = faces(volume)
+    zrest = swap(zrest, "gz", 1)
+    zpair = swap(zpair, "gz", 0)
+    ypair = swap(y, "gy", 0)
+    yrest = swap(y, "gy", 1)
     above = shift(xhi, "gx", True)
-    xlo, front = lax.optimization_barrier((xlo, front))
+    xlo, zrest = lax.optimization_barrier((xlo, zrest))
     below = shift(xlo, "gx", False)
-    halo = (front, back, above, below, first, last)
+    halo = (zpair, zrest, above, below, ypair, yrest)
     near = max(n for n in (1, 2, 4, 8) if bricks % n == 0)
     far = bricks // near
     runs = [[g * near + i for i in range(near)] for g in range(far)]

time: 121 us -> 120 us (level)
  blocking collectives: 98.2 us -> 93.3 us
  starting transfers between devices: 15.3 us -> 19 us
    ppermute x0 -> x4, starting transfers between devices: none -> 13.2 us  [swap(): lax.ppermute(array, axis, [p for i in lower for p in ((i, i + 1), (i + 1,...]
    ppermute x6 -> x2, starting transfers between devices: 15.3 us -> 5.84 us  [shift(): return lax.ppermute(array, axis, pairs)]
    all_to_all x1, blocking collectives: 23.5 us -> 19.8 us  [per_device(): return lay(lax.all_to_all(parts, 'gz', 0, 0, axis_index_groups=runs))]
    all_to_all x1, blocking collectives: 30.6 us -> 28.5 us  [per_device(): parts = lax.all_to_all(parts, 'gz', 0, 0, axis_index_groups=runs)]
where the time goes in v5:
time: 120 us
  blocking collectives  93.3 us (78%)
  starting transfers between devices  19 us (16%)
  Pallas kernels  7.11 us (6%)
    all_to_all x1, blocking collectives, per_device(): parts = lax.all_to_all(parts, 'gz', 0, 0, axis_index_groups=strides)  45 us
    all_to_all x1, blocking collectives, per_device(): parts = lax.all_to_all(parts, 'gz', 0, 0, axis_index_groups=runs)  28.5 us
    all_to_all x1, blocking collectives, per_device(): return lay(lax.all_to_all(parts, 'gz', 0, 0, axis_index_groups=runs))  19.8 us
    ppermute x4, starting transfers between devices, swap(): lax.ppermute(array, axis, [p for i in lower for p in ((i, i + 1), (i + 1,...  13.2 us
    ppermute x2, starting transfers between devices, shift(): return lax.ppermute(array, axis, pairs)  5.84 us
  transfers between devices with their start and end apart: 6, of which 0 were waited for; matrix products, arithmetic and copies ran while one was open for 0% of the time, Pallas kernels for 2%

profile of v5, /device:TPU:6, one launch (start us, length us, event | category | flops | bytes accessed | tf_op | source)
XLA Modules:
  0.0 119.5 jit_solution(10903614059522390276)
XLA Ops:
  0.0 1.9 %faces.1 = (f32[32,128,128]{2,1,0:T(8,128)S(1)}, f32[128,128]{1,0:T(8,128)S(1)}, f32[128,128]{1,0:T(8,128)S(1)}, f32[32,128]{1,0:T(8,128)S(1)}, f32[32,128]{1,0:T(8,128)S(1)}, /*index=5*/f32[128,128]{1,0:T(8,128)S(1)}) custom-call(f32[32,128,128]{2,1,0:T(8,128)} %v_ref.1), custom_call_target="tpu_custom_call" | custom-call | tf_op jit(solution)/shard_map/faces/pallas_call | solution.py:48
  1.9 0.7 collective-permute-start.1
  2.6 7.0 %collective-permute-start = (f32[128,128]{1,0:T(8,128)S(1)}, f32[128,128]{1,0:T(8,128)S(1)}, u32[]{:S(2)}, u32[]{:S(2)}) collective-permute-start(f32[128,128]{1,0:T(8,128)S(1)} %get-tuple-element.22), channel_id=1, source_target_pairs={{0,1},{1,0},{2,3},{3,2},{4,5},{5,4},{6,7},{7,6},{8,9},{9,8},{10,11... | collective-permute-start | bytes 196616 | tf_op jit(solution)/shard_map/ppermute | solution.py:224
  9.6 0.7 collective-permute-start.5
  10.3 4.8 %collective-permute-start.4 = (f32[128,128]{1,0:T(8,128)S(1)}, f32[128,128]{1,0:T(8,128)S(1)}, u32[]{:S(2)}, u32[]{:S(2)}) collective-permute-start(f32[128,128]{1,0:T(8,128)S(1)} %get-tuple-element.28), channel_id=1, source_target_pairs={{0,32},{32,0},{64,96},{96,64},{128,160},{160,128},{192,224},{224,1... | collective-permute-start | bytes 196616 | tf_op jit(solution)/shard_map/ppermute | solution.py:224
  15.1 1.3 %collective-permute-start.2 = (f32[32,128]{1,0:T(8,128)S(1)}, f32[32,128]{1,0:T(8,128)S(1)}, u32[]{:S(2)}, u32[]{:S(2)}) collective-permute-start(f32[32,128]{1,0:T(8,128)S(1)} %get-tuple-element.26), channel_id=1, source_target_pairs={{0,256},{256,512},{512,768},{1,257},{257,513},{513,769},{2,258},{2... | collective-permute-start | bytes 49160 | tf_op jit(solution)/shard_map/ppermute | solution.py:219
  16.4 0.0 collective-permute-done.1.zrest_ref
  16.4 4.5 %collective-permute-start.3 = (f32[32,128]{1,0:T(8,128)S(1)}, f32[32,128]{1,0:T(8,128)S(1)}, u32[]{:S(2)}, u32[]{:S(2)}) collective-permute-start(f32[32,128]{1,0:T(8,128)S(1)} %get-tuple-element.27), channel_id=1, source_target_pairs={{256,0},{512,256},{768,512},{257,1},{513,257},{769,513},{258,2},{5... | collective-permute-start | bytes 49160 | tf_op jit(solution)/shard_map/ppermute | solution.py:219
  21.0 2.1 %weigh.1 = (f32[32,128,128]{2,1,0:T(8,128)S(1)}, f32[32,128,128]{2,1,0:T(8,128)S(1)}, f32[32,128,128]{2,1,0:T(8,128)S(1)}, f32[128,128]{1,0:T(8,128)S(1)}) custom-call(f32[32,128,128]{2,1,0:T(8,128)S(1)} %get-tuple-element.17.v_ref), custom_call_target="tpu_custom_call" | custom-call | flops 15728640 | bytes 8388608 | tf_op jit(solution)/shard_map/weigh/pallas_call | solution.py:90
  23.1 0.0 collective-permute-done.2.xlo_ref
  23.1 0.0 collective-permute-done.zpair_ref
  23.2 0.0 collective-permute-done.5.yrest_ref
  23.2 0.0 collective-permute-done.4.ypair_ref
  23.2 0.0 collective-permute-done.3.xhi_ref
  23.2 2.3 %shade.1 = f32[8,64,128]{2,1,0:T(8,128)S(1)} custom-call(f32[32,128,128]{2,1,0:T(8,128)S(1)} %get-tuple-element.17.v_ref, f32[32,128,128]{2,1,0:T(8,128)S(1)} %get-tuple-element.18.red_ref, f32[32,128,128]{2,1,0:T(8,128)S(1)} %get-tuple-element.19.green_ref, f32[32,128,128]{2,1,0:T(8,128)S(1)} %get-tuple-element.20.blue_ref, ...), custom_call_target="tpu_custom_call" | custom-call | tf_op jit(solution)/shard_map/shade/pallas_call | solution.py:159
  25.5 28.5 %all_to_all.15.parts_ref = f32[8,64,128]{2,1,0:T(8,128)S(1)} all-to-all(f32[8,64,128]{2,1,0:T(8,128)S(1)} %shade.1), channel_id=1, replica_groups={{0,1,2,3,4,5,6,7},{8,9,10,11,12,13,14,15},{16,17,18,19,20,21,22,23},{24..., dimensions={0} | all-to-all | bytes 524288 | tf_op jit(solution)/shard_map/all_to_all | solution.py:244
  54.0 45.0 %all_to_all.16.parts_ref = f32[4,64,128]{2,1,0:T(8,128)S(1)} all-to-all(f32[4,64,128]{2,1,0:T(8,128)S(1)} %merge.2), channel_id=1, replica_groups={{0,8,16,24},{1,9,17,25},{2,10,18,26},{3,11,19,27},{4,12,20,28},{5,13,21..., dimensions={0} | all-to-all | bytes 262144 | tf_op jit(solution)/shard_map/all_to_all | solution.py:246
  99.0 19.8 %all_to_all.17.parts_ref = f32[8,64,128]{2,1,0:T(8,128)S(1)} all-to-all(f32[8,64,128]{2,1,0:T(8,128)S(1)} %merge.3), channel_id=1, replica_groups={{0,1,2,3,4,5,6,7},{8,9,10,11,12,13,14,15},{16,17,18,19,20,21,22,23},{24..., dimensions={0} | all-to-all | bytes 524288 | tf_op jit(solution)/shard_map/all_to_all | solution.py:248
  118.8 0.7 lay.1
  (2 shorter events, 0.0 us)
Async XLA Ops:
  1.9 14.5 %collective-permute-start.1 = (f32[128,128]{1,0:T(8,128)S(1)}, f32[128,128]{1,0:T(8,128)S(1)}, u32[]{:S(2)}, u32[]{:S(2)}) collective-permute-start(f32[128,128]{1,0:T(8,128)S(1)} %get-tuple-element.24), channel_id=1, source_target_pairs={{1,2},{2,1},{3,4},{4,3},{5,6},{6,5},{7,8},{8,7},{9,10},{10,9},{11,... | collective-permute-start | bytes 196616 | tf_op jit(solution)/shard_map/ppermute | solution.py:224
  2.6 20.6 %collective-permute-start = (f32[128,128]{1,0:T(8,128)S(1)}, f32[128,128]{1,0:T(8,128)S(1)}, u32[]{:S(2)}, u32[]{:S(2)}) collective-permute-start(f32[128,128]{1,0:T(8,128)S(1)} %get-tuple-element.22), channel_id=1, source_target_pairs={{0,1},{1,0},{2,3},{3,2},{4,5},{5,4},{6,7},{7,6},{8,9},{9,8},{10,11... | collective-permute-start | bytes 196616 | tf_op jit(solution)/shard_map/ppermute | solution.py:224
  9.6 13.6 %collective-permute-start.5 = (f32[128,128]{1,0:T(8,128)S(1)}, f32[128,128]{1,0:T(8,128)S(1)}, u32[]{:S(2)}, u32[]{:S(2)}) collective-permute-start(f32[128,128]{1,0:T(8,128)S(1)} %get-tuple-element.28), channel_id=1, source_target_pairs={{32,64},{64,32},{96,128},{128,96},{160,192},{192,160},{33,65},{65,... | collective-permute-start | bytes 196616 | tf_op jit(solution)/shard_map/ppermute | solution.py:224
  10.3 12.9 %collective-permute-start.4 = (f32[128,128]{1,0:T(8,128)S(1)}, f32[128,128]{1,0:T(8,128)S(1)}, u32[]{:S(2)}, u32[]{:S(2)}) collective-permute-start(f32[128,128]{1,0:T(8,128)S(1)} %get-tuple-element.28), channel_id=1, source_target_pairs={{0,32},{32,0},{64,96},{96,64},{128,160},{160,128},{192,224},{224,1... | collective-permute-start | bytes 196616 | tf_op jit(solution)/shard_map/ppermute | solution.py:224
  15.1 8.0 %collective-permute-start.2 = (f32[32,128]{1,0:T(8,128)S(1)}, f32[32,128]{1,0:T(8,128)S(1)}, u32[]{:S(2)}, u32[]{:S(2)}) collective-permute-start(f32[32,128]{1,0:T(8,128)S(1)} %get-tuple-element.26), channel_id=1, source_target_pairs={{0,256},{256,512},{512,768},{1,257},{257,513},{513,769},{2,258},{2... | collective-permute-start | bytes 49160 | tf_op jit(solution)/shard_map/ppermute | solution.py:219
  16.4 6.8 %collective-permute-start.3 = (f32[32,128]{1,0:T(8,128)S(1)}, f32[32,128]{1,0:T(8,128)S(1)}, u32[]{:S(2)}, u32[]{:S(2)}) collective-permute-start(f32[32,128]{1,0:T(8,128)S(1)} %get-tuple-element.27), channel_id=1, source_target_pairs={{256,0},{512,256},{768,512},{257,1},{513,257},{769,513},{258,2},{5... | collective-permute-start | bytes 49160 | tf_op jit(solution)/shard_map/ppermute | solution.py:219

commit v6 on v5

--- a/solution.py
+++ b/solution.py
@@ -103,11 +103,12 @@
     odd_y = lax.rem(lax.axis_index("gy"), 2) == 1
     nz, nx, ny = v_ref.shape
     pieces = out_ref.shape[0]
-    height, unroll = nx // pieces, 16
+    height, unroll = 16, 16
+    tall = nx // pieces
     col = lax.broadcasted_iota(jnp.int32, (height, ny), 1)
     line = lax.broadcasted_iota(jnp.int32, (height, ny), 0)
     odd = col % 2 == 1
-    for block in range(pieces):
+    for block in range(nx // height):
         start = block * height
         rows = slice(start, start + height)
         pair, rest = ypair_ref[rows, :], yrest_ref[rows, :]
@@ -121,7 +122,7 @@
                 above = jnp.where(line == 0, xlo_ref[pl.ds(z, 1), :], pltpu.roll(cur, 1, 0))
             else:
                 above = v_ref[z, start - 1 : start - 1 + height, :]
-            if block == pieces - 1:
+            if start + height == nx:
                 below = jnp.where(line == height - 1, xhi_ref[pl.ds(z, 1), :], pltpu.roll(cur, height - 1, 0))
             else:
                 below = v_ref[z, start + 1 : start + 1 + height, :]
@@ -151,7 +152,8 @@
             sums = step(z, prev, cur, new, sums)
             prev, cur = cur, new
         for c, value in enumerate((*sums, clear_ref[rows, :])):
-            out_ref[block, c * height : (c + 1) * height, :] = value
+            place = c * tall + start % tall
+            out_ref[start // tall, place : place + height, :] = value
 
 
 def shade(volume, weights, halo, pieces):
@@ -166,8 +168,8 @@
     )(volume, *weights, *halo)
 
 
-def merge_kernel(final, parts_ref, out_ref):
-    count, rows, ny = parts_ref.shape
+def composite(parts_ref):
+    count, rows, _ = parts_ref.shape
     part = rows // 4
     clear = parts_ref[0, 3 * part :, :]
     total = [parts_ref[0, c * part : (c + 1) * part, :] for c in range(3)]
@@ -175,41 +177,48 @@
         for c in range(3):
             total[c] = total[c] + clear * parts_ref[k, c * part : (c + 1) * part, :]
         clear = clear * parts_ref[k, 3 * part :, :]
-    total.append(1.0 - clear if final else clear)
+    return total, clear
+
+
+def cut_kernel(parts_ref, out_ref):
+    total, clear = composite(parts_ref)
+    part = out_ref.shape[1] // 4
     for k in range(out_ref.shape[0]):
-        for c in range(4):
-            out_ref[k, c * part : (c + 1) * part, :] = total[c]
-
-
-def merge(parts, copies, final):
-    _, rows, ny = parts.shape
-    return pl.pallas_call(
-        functools.partial(merge_kernel, final),
-        out_shape=jax.ShapeDtypeStruct((copies, rows, ny), jnp.float32),
+        for c, value in enumerate((*total, clear)):
+            out_ref[k, c * part : (c + 1) * part, :] = value[k * part : (k + 1) * part, :]
+
+
+def final_kernel(parts_ref, out_ref):
+    total, clear = composite(parts_ref)
+    part = out_ref.shape[1] // 4
+    for k in range(out_ref.shape[0]):
+        for c, value in enumerate((*total, 1.0 - clear)):
+            out_ref[k, c * part : (c + 1) * part, :] = value
+
+
+def repeat_kernel(parts_ref, out_ref):
+    for k in range(out_ref.shape[0]):
+        out_ref[k] = parts_ref[...]
+
+
+def lay_kernel(parts_ref, out_ref):
+    runs, count, rows, _ = parts_ref.shape
+    part = rows // 4
+    for r in range(runs):
+        for k in range(count):
+            for c in range(4):
+                row = (r * count + k) * part
+                out_ref[c, row : row + part, :] = parts_ref[r, k, c * part : (c + 1) * part, :]
+
+
+def small(kernel, shape, parts):
+    return pl.pallas_call(
+        kernel,
+        out_shape=jax.ShapeDtypeStruct(shape, jnp.float32),
         in_specs=[whole()],
         out_specs=whole(),
         compiler_params=pltpu.CompilerParams(vmem_limit_bytes=8 << 20),
-        name="merge",
-    )(parts)
-
-
-def lay_kernel(parts_ref, out_ref):
-    count, rows, ny = parts_ref.shape
-    part = rows // 4
-    for k in range(count):
-        for c in range(4):
-            out_ref[c, k * part : (k + 1) * part, :] = parts_ref[k, c * part : (c + 1) * part, :]
-
-
-def lay(parts):
-    count, rows, ny = parts.shape
-    return pl.pallas_call(
-        lay_kernel,
-        out_shape=jax.ShapeDtypeStruct((4, count * rows // 4, ny), jnp.float32),
-        in_specs=[whole()],
-        out_specs=whole(),
-        compiler_params=pltpu.CompilerParams(vmem_limit_bytes=8 << 20),
-        name="lay",
+        name=kernel.__name__,
     )(parts)
 
 
@@ -236,16 +245,21 @@
     xlo, zrest = lax.optimization_barrier((xlo, zrest))
     below = shift(xlo, "gx", False)
     halo = (zpair, zrest, above, below, ypair, yrest)
-    near = max(n for n in (1, 2, 4, 8) if bricks % n == 0)
+    nx, ny = volume.shape[1:]
+    near = 4
     far = bricks // near
     runs = [[g * near + i for i in range(near)] for g in range(far)]
     strides = [[g * near + i for g in range(far)] for i in range(near)]
+    piece = (far, 4 * nx // bricks, ny)
     parts = shade(own, weigh(own, depth_cells), halo, near)
     parts = lax.all_to_all(parts, "gz", 0, 0, axis_index_groups=runs)
-    parts = merge(parts, far, False)
+    parts = small(cut_kernel, piece, parts)
     parts = lax.all_to_all(parts, "gz", 0, 0, axis_index_groups=strides)
-    parts = merge(parts, near, True)
-    return lay(lax.all_to_all(parts, "gz", 0, 0, axis_index_groups=runs))
+    parts = small(final_kernel, piece, parts)
+    parts = lax.all_to_all(parts, "gz", 0, 0, axis_index_groups=strides)
+    parts = small(repeat_kernel, (near, *piece), parts)
+    parts = lax.all_to_all(parts, "gz", 0, 0, axis_index_groups=runs)
+    return small(lay_kernel, (4, nx, ny), parts)
 
 
 def solution(mesh):

time: 120 us -> 125 us (1.042)
  blocking collectives: 93.3 us -> 97.9 us
    all_to_all x1 -> x2, blocking collectives: 45 us -> 73.6 us  [per_device(): parts = lax.all_to_all(parts, 'gz', 0, 0, axis_index_groups=strides)]
    all_to_all x1 -> x0, blocking collectives: 19.8 us -> none  [per_device(): return lay(lax.all_to_all(parts, 'gz', 0, 0, axis_index_groups=runs))]
    all_to_all x1 -> x2, blocking collectives: 28.5 us -> 24.3 us  [per_device(): parts = lax.all_to_all(parts, 'gz', 0, 0, axis_index_groups=runs)]
where the time goes in v6:
time: 125 us; the launch traced here: 124 us
  blocking collectives  97.9 us (78%)
  starting transfers between devices  19 us (15%)
  Pallas kernels  7.15 us (6%)
    all_to_all x2, blocking collectives, per_device(): parts = lax.all_to_all(parts, 'gz', 0, 0, axis_index_groups=strides)  73.6 us
    all_to_all x2, blocking collectives, per_device(): parts = lax.all_to_all(parts, 'gz', 0, 0, axis_index_groups=runs)  24.3 us
    ppermute x4, starting transfers between devices, swap(): lax.ppermute(array, axis, [p for i in lower for p in ((i, i + 1), (i + 1,...  13.2 us
    ppermute x2, starting transfers between devices, shift(): return lax.ppermute(array, axis, pairs)  5.84 us
  transfers between devices with their start and end apart: 6, of which 0 were waited for; matrix products, arithmetic and copies ran while one was open for 0% of the time, Pallas kernels for 2%

profile of v6, /device:TPU:6, one launch (start us, length us, event | category | flops | bytes accessed | tf_op | source)
XLA Modules:
  0.0 124.2 jit_solution(13598587820779866832)
XLA Ops:
  0.0 1.9 %faces.1 = (f32[32,128,128]{2,1,0:T(8,128)S(1)}, f32[128,128]{1,0:T(8,128)S(1)}, f32[128,128]{1,0:T(8,128)S(1)}, f32[32,128]{1,0:T(8,128)S(1)}, f32[32,128]{1,0:T(8,128)S(1)}, /*index=5*/f32[128,128]{1,0:T(8,128)S(1)}) custom-call(f32[32,128,128]{2,1,0:T(8,128)} %v_ref.1), custom_call_target="tpu_custom_call" | custom-call | tf_op jit(solution)/shard_map/faces/pallas_call | solution.py:48
  1.9 0.7 collective-permute-start.1
  2.6 7.0 %collective-permute-start = (f32[128,128]{1,0:T(8,128)S(1)}, f32[128,128]{1,0:T(8,128)S(1)}, u32[]{:S(2)}, u32[]{:S(2)}) collective-permute-start(f32[128,128]{1,0:T(8,128)S(1)} %get-tuple-element.22), channel_id=1, source_target_pairs={{0,1},{1,0},{2,3},{3,2},{4,5},{5,4},{6,7},{7,6},{8,9},{9,8},{10,11... | collective-permute-start | bytes 196616 | tf_op jit(solution)/shard_map/ppermute | solution.py:233
  9.6 0.7 collective-permute-start.5
  10.3 4.8 %collective-permute-start.4 = (f32[128,128]{1,0:T(8,128)S(1)}, f32[128,128]{1,0:T(8,128)S(1)}, u32[]{:S(2)}, u32[]{:S(2)}) collective-permute-start(f32[128,128]{1,0:T(8,128)S(1)} %get-tuple-element.28), channel_id=1, source_target_pairs={{0,32},{32,0},{64,96},{96,64},{128,160},{160,128},{192,224},{224,1... | collective-permute-start | bytes 196616 | tf_op jit(solution)/shard_map/ppermute | solution.py:233
  15.1 1.3 %collective-permute-start.2 = (f32[32,128]{1,0:T(8,128)S(1)}, f32[32,128]{1,0:T(8,128)S(1)}, u32[]{:S(2)}, u32[]{:S(2)}) collective-permute-start(f32[32,128]{1,0:T(8,128)S(1)} %get-tuple-element.26), channel_id=1, source_target_pairs={{0,256},{256,512},{512,768},{1,257},{257,513},{513,769},{2,258},{2... | collective-permute-start | bytes 49160 | tf_op jit(solution)/shard_map/ppermute | solution.py:228
  16.4 0.0 collective-permute-done.1.zrest_ref
  16.4 4.5 %collective-permute-start.3 = (f32[32,128]{1,0:T(8,128)S(1)}, f32[32,128]{1,0:T(8,128)S(1)}, u32[]{:S(2)}, u32[]{:S(2)}) collective-permute-start(f32[32,128]{1,0:T(8,128)S(1)} %get-tuple-element.27), channel_id=1, source_target_pairs={{256,0},{512,256},{768,512},{257,1},{513,257},{769,513},{258,2},{5... | collective-permute-start | bytes 49160 | tf_op jit(solution)/shard_map/ppermute | solution.py:228
  21.0 2.1 %weigh.1 = (f32[32,128,128]{2,1,0:T(8,128)S(1)}, f32[32,128,128]{2,1,0:T(8,128)S(1)}, f32[32,128,128]{2,1,0:T(8,128)S(1)}, f32[128,128]{1,0:T(8,128)S(1)}) custom-call(f32[32,128,128]{2,1,0:T(8,128)S(1)} %get-tuple-element.17.v_ref), custom_call_target="tpu_custom_call" | custom-call | flops 15728640 | bytes 8388608 | tf_op jit(solution)/shard_map/weigh/pallas_call | solution.py:90
  23.1 0.0 collective-permute-done.2.xlo_ref
  23.1 0.0 collective-permute-done.zpair_ref
  23.2 0.0 collective-permute-done.5.yrest_ref
  23.2 0.0 collective-permute-done.4.ypair_ref
  23.2 0.0 collective-permute-done.3.xhi_ref
  23.2 2.3 %shade.1 = f32[4,128,128]{2,1,0:T(8,128)S(1)} custom-call(f32[32,128,128]{2,1,0:T(8,128)S(1)} %get-tuple-element.17.v_ref, f32[32,128,128]{2,1,0:T(8,128)S(1)} %get-tuple-element.18.red_ref, f32[32,128,128]{2,1,0:T(8,128)S(1)} %get-tuple-element.19.green_ref, f32[32,128,128]{2,1,0:T(8,128)S(1)} %get-tuple-element.20.blue_ref, ...), custom_call_target="tpu_custom_call" | custom-call | tf_op jit(solution)/shard_map/shade/pallas_call | solution.py:161
  25.5 14.0 %all_to_all.20.parts_ref = f32[4,128,128]{2,1,0:T(8,128)S(1)} all-to-all(f32[4,128,128]{2,1,0:T(8,128)S(1)} %shade.1), channel_id=1, replica_groups={{0,1,2,3},{4,5,6,7},{8,9,10,11},{12,13,14,15},{16,17,18,19},{20,21,22,2..., dimensions={0} | all-to-all | bytes 524288 | tf_op jit(solution)/shard_map/all_to_all | solution.py:255
  39.5 47.0 %all_to_all.21.parts_ref = f32[8,16,128]{2,1,0:T(8,128)S(1)} all-to-all(f32[8,16,128]{2,1,0:T(8,128)S(1)} %cut_kernel.1), channel_id=1, replica_groups={{0,4,8,12,16,20,24,28},{1,5,9,13,17,21,25,29},{2,6,10,14,18,22,26,30},{..., dimensions={0} | all-to-all | bytes 131072 | tf_op jit(solution)/shard_map/all_to_all | solution.py:257
  86.6 26.6 %all_to_all.22.parts_ref = f32[8,16,128]{2,1,0:T(8,128)S(1)} all-to-all(f32[8,16,128]{2,1,0:T(8,128)S(1)} %final_kernel.1), channel_id=1, replica_groups={{0,4,8,12,16,20,24,28},{1,5,9,13,17,21,25,29},{2,6,10,14,18,22,26,30},{..., dimensions={0} | all-to-all | bytes 131072 | tf_op jit(solution)/shard_map/all_to_all | solution.py:259
  113.2 10.3 %all_to_all.23.parts_ref = f32[4,8,16,128]{3,2,1,0:T(8,128)S(1)} all-to-all(f32[4,8,16,128]{3,2,1,0:T(8,128)S(1)} %repeat_kernel.1), channel_id=1, replica_groups={{0,1,2,3},{4,5,6,7},{8,9,10,11},{12,13,14,15},{16,17,18,19},{20,21,22,2..., dimensions={0} | all-to-all | bytes 524288 | tf_op jit(solution)/shard_map/all_to_all | solution.py:261
  123.5 0.7 lay_kernel.1
  (3 shorter events, 0.1 us)
Async XLA Ops:
  1.9 14.5 %collective-permute-start.1 = (f32[128,128]{1,0:T(8,128)S(1)}, f32[128,128]{1,0:T(8,128)S(1)}, u32[]{:S(2)}, u32[]{:S(2)}) collective-permute-start(f32[128,128]{1,0:T(8,128)S(1)} %get-tuple-element.24), channel_id=1, source_target_pairs={{1,2},{2,1},{3,4},{4,3},{5,6},{6,5},{7,8},{8,7},{9,10},{10,9},{11,... | collective-permute-start | bytes 196616 | tf_op jit(solution)/shard_map/ppermute | solution.py:233
  2.6 20.6 %collective-permute-start = (f32[128,128]{1,0:T(8,128)S(1)}, f32[128,128]{1,0:T(8,128)S(1)}, u32[]{:S(2)}, u32[]{:S(2)}) collective-permute-start(f32[128,128]{1,0:T(8,128)S(1)} %get-tuple-element.22), channel_id=1, source_target_pairs={{0,1},{1,0},{2,3},{3,2},{4,5},{5,4},{6,7},{7,6},{8,9},{9,8},{10,11... | collective-permute-start | bytes 196616 | tf_op jit(solution)/shard_map/ppermute | solution.py:233
  9.6 13.6 %collective-permute-start.5 = (f32[128,128]{1,0:T(8,128)S(1)}, f32[128,128]{1,0:T(8,128)S(1)}, u32[]{:S(2)}, u32[]{:S(2)}) collective-permute-start(f32[128,128]{1,0:T(8,128)S(1)} %get-tuple-element.28), channel_id=1, source_target_pairs={{32,64},{64,32},{96,128},{128,96},{160,192},{192,160},{33,65},{65,... | collective-permute-start | bytes 196616 | tf_op jit(solution)/shard_map/ppermute | solution.py:233
  10.3 12.9 %collective-permute-start.4 = (f32[128,128]{1,0:T(8,128)S(1)}, f32[128,128]{1,0:T(8,128)S(1)}, u32[]{:S(2)}, u32[]{:S(2)}) collective-permute-start(f32[128,128]{1,0:T(8,128)S(1)} %get-tuple-element.28), channel_id=1, source_target_pairs={{0,32},{32,0},{64,96},{96,64},{128,160},{160,128},{192,224},{224,1... | collective-permute-start | bytes 196616 | tf_op jit(solution)/shard_map/ppermute | solution.py:233
  15.1 8.0 %collective-permute-start.2 = (f32[32,128]{1,0:T(8,128)S(1)}, f32[32,128]{1,0:T(8,128)S(1)}, u32[]{:S(2)}, u32[]{:S(2)}) collective-permute-start(f32[32,128]{1,0:T(8,128)S(1)} %get-tuple-element.26), channel_id=1, source_target_pairs={{0,256},{256,512},{512,768},{1,257},{257,513},{513,769},{2,258},{2... | collective-permute-start | bytes 49160 | tf_op jit(solution)/shard_map/ppermute | solution.py:228
  16.4 6.8 %collective-permute-start.3 = (f32[32,128]{1,0:T(8,128)S(1)}, f32[32,128]{1,0:T(8,128)S(1)}, u32[]{:S(2)}, u32[]{:S(2)}) collective-permute-start(f32[32,128]{1,0:T(8,128)S(1)} %get-tuple-element.27), channel_id=1, source_target_pairs={{256,0},{512,256},{768,512},{257,1},{513,257},{769,513},{258,2},{5... | collective-permute-start | bytes 49160 | tf_op jit(solution)/shard_map/ppermute | solution.py:228
